TPU v7x, 32 devices: a whole 2x2x4 slice. The times are simulated.
32 devices in a mesh: dp: 4 (over z), seq: 8 (over y, x, core).
Axes of the slice: x: 2, y: 2, z: 4, core: 2. Of those that a mesh axis runs over, the one named last changes fastest.
Arguments:
- frames_in: bfloat16 [4, 4096, 1024], P('dp', 'seq'), may hold values from -16 to 16
- memory_in: bfloat16 [4, 32, 1024], P('dp', 'seq'), may hold values from -6 to 6
- w_query: bfloat16 [1024, 1024], P(None, 'dp'), may hold values from -1 to 1
- w_key: bfloat16 [1024, 1024], P(None, 'dp'), may hold values from -1 to 1
- w_value: bfloat16 [1024, 1024], P(None, 'dp'), may hold values from -0.1875 to 0.1875
- lengths: int32 [4], P('dp'), may hold values from 1024 to 4096, as said below
Outputs:
- context: bfloat16 [4, 4096, 1024], P('dp', 'seq')
- memory_out: bfloat16 [4, 32, 1024], P('dp', 'seq')
Inputs may be any that keep to these rules, and one draw needn't show every extreme that they name: `lengths`: some utterance has all 4096 frames live; every utterance has at least a quarter of them.
All inputs are finite; a program needn't handle non-finite values.
Results may differ from a plain program's by a relative error of at most 0.0071.
Values may be sent and summed in bfloat16 or wider, within the bound.
No kernel may reach another device: no remote copies, remote signals or barrier semaphores. Data moves between devices by JAX's collectives and lax.ppermute only.
A program may use at most 64 MiB of HBM per device.

v0:
```python
import jax
import jax.numpy as jnp
from jax import lax
from jax.sharding import PartitionSpec as P

HEADS = 16
LEFT = 128
RIGHT = 32


def passed_along(block, axis, distance):
    devices = range(lax.axis_size(axis))
    route = [(i - distance, i) for i in devices if i - distance in devices]
    return lax.ppermute(block, axis, route)


def attend(queries, keys, values, key_live, scale):
    utt_count, n_query, feat_width = queries.shape
    n_key = keys.shape[1]
    q_heads = queries.reshape(utt_count, n_query, HEADS, -1)
    k_heads = keys.reshape(utt_count, n_key, HEADS, -1)
    v_heads = values.reshape(utt_count, n_key, HEADS, -1)
    scores = (
        jnp.einsum("bqhe,bkhe->bhqk", q_heads, k_heads, preferred_element_type=jnp.float32) * scale
    )
    scores = jnp.where(key_live[:, None, None, :], scores, -1e30)
    row_max = jnp.max(scores, axis=-1, keepdims=True)
    probs = jnp.exp(scores - row_max)
    weights = (probs / jnp.sum(probs, axis=-1, keepdims=True)).astype(jnp.bfloat16)
    mixed = jnp.einsum("bhqk,bkhe->bqhe", weights, v_heads, preferred_element_type=jnp.float32)
    return mixed.reshape(utt_count, n_query, feat_width)


def local(frames_in, memory_in, w_query, w_key, w_value, lengths):
    utt_count, row_count, feat_width = frames_in.shape
    seg_dev = memory_in.shape[1]
    seg_len = row_count // seg_dev
    key_span = LEFT + seg_len + RIGHT
    scale = float(feat_width // HEADS) ** (-0.5)
    seq_index = lax.axis_index("seq")
    row_base = seq_index * row_count
    frame_start = 0
    bank_rows = lax.all_gather(memory_in, "seq", axis=1, tiled=True)
    row_pos = row_base + jnp.arange(row_count, dtype=jnp.int32)
    live_mask = row_pos[None, :] < lengths[:, None]
    live_blocks = live_mask.reshape(utt_count, seg_dev, seg_len)
    masked_sums = jnp.einsum(
        "bnsd,bns->bnd",
        frames_in.reshape(utt_count, seg_dev, seg_len, feat_width),
        live_blocks.astype(jnp.bfloat16),
        preferred_element_type=jnp.float32,
    )
    counts = jnp.sum(live_blocks.astype(jnp.float32), axis=2)
    summary = (masked_sums / jnp.maximum(counts, 1.0)[:, :, None]).astype(jnp.bfloat16)
    n_frame = frames_in.shape[1]
    all_rows = jnp.concatenate([frames_in, summary, bank_rows], axis=1)
    n_total = all_rows.shape[1]
    flat_rows = all_rows.reshape(utt_count * n_total, feat_width)

    def project_one(piece):
        return jnp.dot(flat_rows, piece, preferred_element_type=jnp.float32).astype(jnp.bfloat16)

    q_flat = project_one(lax.all_gather(w_query, "dp", axis=1, tiled=True))
    k_flat = project_one(lax.all_gather(w_key, "dp", axis=1, tiled=True))
    v_flat = project_one(lax.all_gather(w_value, "dp", axis=1, tiled=True))
    q_all = q_flat.reshape(utt_count, n_total, feat_width)
    k_all = k_flat.reshape(utt_count, n_total, feat_width)
    v_all = v_flat.reshape(utt_count, n_total, feat_width)
    q_frames = q_all[:, frame_start : frame_start + row_count]
    q_summary = q_all[:, n_frame : n_frame + seg_dev]
    bank_keys = k_all[:, n_frame + seg_dev :]
    bank_values = v_all[:, n_frame + seg_dev :]
    k_own = k_all[:, :row_count]
    v_own = v_all[:, :row_count]
    k_before, v_before = passed_along(
        (k_own[:, row_count - LEFT :], v_own[:, row_count - LEFT :]), "seq", 1
    )
    k_after, v_after = passed_along((k_own[:, :RIGHT], v_own[:, :RIGHT]), "seq", -1)
    k_ext = jnp.concatenate([k_before, k_own, k_after], axis=1)
    v_ext = jnp.concatenate([v_before, v_own, v_after], axis=1)
    bank_count = bank_keys.shape[1]
    bank_index = jnp.arange(bank_count, dtype=jnp.int32)
    bank_ready = bank_index[None, :] * seg_len < lengths[:, None]

    def one_segment(seg_index):
        global_seg = seq_index * seg_dev + seg_index
        q_rows = lax.dynamic_slice_in_dim(q_frames, seg_index * seg_len, seg_len, 1)
        q_sum = lax.dynamic_slice_in_dim(q_summary, seg_index, 1, 1)
        queries = jnp.concatenate([q_rows, q_sum], axis=1)
        k_window = lax.dynamic_slice_in_dim(k_ext, seg_index * seg_len, key_span, 1)
        v_window = lax.dynamic_slice_in_dim(v_ext, seg_index * seg_len, key_span, 1)
        frame_pos = row_base - LEFT + seg_index * seg_len + jnp.arange(key_span, dtype=jnp.int32)
        frame_live = (frame_pos[None, :] >= 0) & (frame_pos[None, :] < lengths[:, None])
        key_live = jnp.concatenate(
            [bank_ready & (bank_index < global_seg)[None, :], frame_live], axis=1
        )
        keys = jnp.concatenate([bank_keys, k_window], axis=1)
        values = jnp.concatenate([bank_values, v_window], axis=1)
        return attend(queries, keys, values, key_live, scale)

    attended = lax.map(one_segment, jnp.arange(seg_dev, dtype=jnp.int32))
    frame_part = (
        attended[:, :, :seg_len].transpose(1, 0, 2, 3).reshape(utt_count, row_count, feat_width)
    )
    context = (frame_part * live_mask[:, :, None].astype(jnp.float32)).astype(jnp.bfloat16)
    memory_out = attended[:, :, seg_len].transpose(1, 0, 2).astype(jnp.bfloat16)
    return (context, memory_out)


def solution(mesh):
    placed = (
        P("dp", "seq", None),
        P("dp", "seq", None),
        P(None, "dp"),
        P(None, "dp"),
        P(None, "dp"),
        P("dp"),
    )
    return jax.shard_map(
        local,
        mesh=mesh,
        in_specs=placed,
        out_specs=(P("dp", "seq", None), P("dp", "seq", None)),
        check_vma=False,
    )
```

profile of v0, /device:TPU:3, one launch (start us, length us, event | category | flops | bytes accessed | tf_op | source)
XLA Modules:
  0.0 252.9 jit_solution(9510433819351743117)
XLA Ops:
  10.8 9.7 %all_gather.12 = bf16[1,32,1024]{2,0,1:T(2,128)(2,1)S(1)} all-gather(bf16[1,4,1024]{2,0,1:T(2,128)(2,1)S(1)} %copy.26), channel_id=1, replica_groups=mesh['dp'=4,'seq'=8] {'seq'}, dimensions={1}, use_global_device_ids=true | all-gather | bytes 73728 | tf_op jit(solution)/shard_map/all_gather | solution.py:43
  22.3 34.8 %all-gather.4.cloned.1.call-done = bf16[1024,1024]{1,0:T(8,128)(2,1)} async-done(((bf16[1024,256]{1,0:T(8,128)(2,1)}), bf16[1024,1024]{1,0:T(8,128)(2,1)}) %all-gather.4.cloned.1.call-update) | async-done | bytes 2097168 | tf_op jit(solution)/shard_map/all_gather | solution.py:65
  57.1 2.9 %fusion.15 = bf16[1,548,1024]{2,1,0:T(8,128)(2,1)S(1)} fusion(bf16[1024,1024]{1,0:T(8,128)(2,1)} %all-gather.4.cloned.1.call-done, bf16[1,32,1024]{2,1,0:T(8,128)(2,1)S(1)} %copy.27, bf16[1,4,1024]{2,1,0:T(4,128)(2,1)S(1)} %fusion.20, bf16[1,512,1024]{2,1,0:T(8,128)(2,1)S(1)} %copy-done.3), kind=kOutput, calls=%fused_computation.30 | convolution fusion | flops 1153167360 | bytes 4341760 | tf_op jit(solution)/shard_map/dot_general | solution.py:61
  61.4 2.5 collective-permute-start.1
  64.0 3.9 %collective-permute-start = (bf16[1,128,1024]{2,1,0:T(8,128)(2,1)}, bf16[1,128,1024]{2,1,0:T(8,128)(2,1)}, u32[]{:S(2)}, u32[]{:S(2)}) collective-permute-start(bf16[1,128,1024]{2,1,0:T(8,128)(2,1)} %slice.53), channel_id=1, source_target_pairs={{0,1},{1,2},{2,3},{3,4},{4,5},{5,6},{6,7},{8,9},{9,10},{10,11},{11... | collective-permute-start | bytes 786440 | tf_op jit(solution)/shard_map/ppermute | solution.py:14
  67.9 35.3 %all-gather.8.cloned.1.call-done = bf16[1024,1024]{1,0:T(8,128)(2,1)} async-done(((bf16[1024,256]{1,0:T(8,128)(2,1)}), bf16[1024,1024]{1,0:T(8,128)(2,1)}) %all-gather.8.cloned.1.call-update) | async-done | bytes 2097168 | tf_op jit(solution)/shard_map/all_gather | solution.py:64
  103.1 2.9 %fusion.17 = bf16[1,548,1024]{2,1,0:T(8,128)(2,1)S(1)} fusion(bf16[1024,1024]{1,0:T(8,128)(2,1)} %all-gather.8.cloned.1.call-done, bf16[1,32,1024]{2,1,0:T(8,128)(2,1)S(1)} %copy.27, bf16[1,4,1024]{2,1,0:T(4,128)(2,1)S(1)} %fusion.20, bf16[1,512,1024]{2,1,0:T(8,128)(2,1)S(1)} %copy-done.3), kind=kOutput, calls=%fused_computation.32 | convolution fusion | flops 1153167360 | bytes 4341760 | tf_op jit(solution)/shard_map/dot_general | solution.py:61
  106.9 3.6 %collective-permute-start.2 = (bf16[1,128,1024]{2,1,0:T(8,128)(2,1)}, bf16[1,128,1024]{2,1,0:T(8,128)(2,1)}, u32[]{:S(2)}, u32[]{:S(2)}) collective-permute-start(bf16[1,128,1024]{2,1,0:T(8,128)(2,1)} %slice.59), channel_id=1, source_target_pairs={{0,1},{1,2},{2,3},{3,4},{4,5},{5,6},{6,7},{8,9},{9,10},{10,11},{11... | collective-permute-start | bytes 786440 | tf_op jit(solution)/shard_map/ppermute | solution.py:14
  110.5 38.7 %all-gather.6.cloned.1.call-done = bf16[1024,1024]{1,0:T(8,128)(2,1)} async-done(((bf16[1024,256]{1,0:T(8,128)(2,1)}), bf16[1024,1024]{1,0:T(8,128)(2,1)}) %all-gather.6.cloned.1.call-update) | async-done | bytes 2097168 | tf_op jit(solution)/shard_map/all_gather | solution.py:63
  149.2 2.9 %fusion.16 = bf16[1,548,1024]{2,1,0:T(8,128)(2,1)S(1)} fusion(bf16[1024,1024]{1,0:T(8,128)(2,1)} %all-gather.6.cloned.1.call-done, bf16[1,32,1024]{2,1,0:T(8,128)(2,1)S(1)} %copy.27, bf16[1,4,1024]{2,1,0:T(4,128)(2,1)S(1)} %fusion.20, bf16[1,512,1024]{2,1,0:T(8,128)(2,1)S(1)} %copy-done.3), kind=kOutput, calls=%fused_computation.31 | convolution fusion | flops 1153167360 | bytes 4341760 | tf_op jit(solution)/shard_map/dot_general | solution.py:61
  154.2 2.7 %collective-permute-start.3 = (bf16[1,32,1024]{2,1,0:T(8,128)(2,1)S(1)}, bf16[1,32,1024]{2,1,0:T(8,128)(2,1)S(1)}, u32[]{:S(2)}, u32[]{:S(2)}) collective-permute-start(bf16[1,32,1024]{2,1,0:T(8,128)(2,1)S(1)} %get-tuple-element.266), channel_id=1, source_target_pairs={{1,0},{2,1},{3,2},{4,3},{5,4},{6,5},{7,6},{9,8},{10,9},{11,10},{12... | collective-permute-start | bytes 196616 | tf_op jit(solution)/shard_map/ppermute | solution.py:14
  160.9 2.2 pad_maximum_fusion.4
  163.1 72.8 %while.13 = (s32[]{:T(128)}, f32[4,1,129,1024]{2,3,1,0:T(8,128)}, s32[4]{0:T(128)S(1)}, bf16[1,672,1024]{2,1,0:T(8,128)(2,1)S(1)}, bf16[1,32,1024]{1,2,0:T(8,128...) while((s32[]{:T(128)}, f32[4,1,129,1024]{2,3,1,0:T(8,128)}, ...), condition=%wide.region_4.5_spmd.clone, body=%wide.region_1.4_spmd.clone.sunk | while | flops 176197520 | bytes 28918032 | solution.py:101
  173.7 3.0 %fusion.45 = (f32[16,129]{1,0:T(8,128)S(1)}, f32[16,129,320]{2,1,0:T(8,128)}) fusion(pred[320]{0:T(512)(128)(4,1)S(1)} %add_reduce_fusion.2, bf16[129,16,64]{0,2,1:T(8,128)(2,1)S(1)} %bitcast.76, bf16[320,16,64]{0,2,1:T(8,128)(2,1)S(1)} %bitcast.75), kind=kOutput, calls=%fused_computation.50.clone.1 | convolution fusion | flops 87183680 | bytes 3570048 | tf_op jit(solution)/shard_map/while/body/eval_jaxpr/sub | solution.py:28
  176.7 2.9 %fusion.46 = f32[16,64,129]{2,1,0:T(8,128)S(1)} fusion(bf16[320,16,64]{0,2,1:T(8,128)(2,1)S(1)} %bitcast.74, f32[16,129,320]{2,1,0:T(8,128)} %get-tuple-element.354, f32[16,129]{1,0:T(8,128)S(1)} %get-tuple-element.355), kind=kOutput, calls=%fused_computation.9.clone.1 | convolution fusion | flops 85862400 | bytes 3833920 | tf_op jit(solution)/shard_map/while/body/eval_jaxpr/bhqk,bkhe->bqhe/dot_general | solution.py:30
  191.9 3.0 %fusion.45 = (f32[16,129]{1,0:T(8,128)S(1)}, f32[16,129,320]{2,1,0:T(8,128)}) fusion(pred[320]{0:T(512)(128)(4,1)S(1)} %add_reduce_fusion.2, bf16[129,16,64]{0,2,1:T(8,128)(2,1)S(1)} %bitcast.76, bf16[320,16,64]{0,2,1:T(8,128)(2,1)S(1)} %bitcast.75), kind=kOutput, calls=%fused_computation.50.clone.1 | convolution fusion | flops 87183680 | bytes 3570048 | tf_op jit(solution)/shard_map/while/body/eval_jaxpr/sub | solution.py:28
  194.9 2.9 %fusion.46 = f32[16,64,129]{2,1,0:T(8,128)S(1)} fusion(bf16[320,16,64]{0,2,1:T(8,128)(2,1)S(1)} %bitcast.74, f32[16,129,320]{2,1,0:T(8,128)} %get-tuple-element.354, f32[16,129]{1,0:T(8,128)S(1)} %get-tuple-element.355), kind=kOutput, calls=%fused_computation.9.clone.1 | convolution fusion | flops 85862400 | bytes 3833920 | tf_op jit(solution)/shard_map/while/body/eval_jaxpr/bhqk,bkhe->bqhe/dot_general | solution.py:30
  210.1 3.0 %fusion.45 = (f32[16,129]{1,0:T(8,128)S(1)}, f32[16,129,320]{2,1,0:T(8,128)}) fusion(pred[320]{0:T(512)(128)(4,1)S(1)} %add_reduce_fusion.2, bf16[129,16,64]{0,2,1:T(8,128)(2,1)S(1)} %bitcast.76, bf16[320,16,64]{0,2,1:T(8,128)(2,1)S(1)} %bitcast.75), kind=kOutput, calls=%fused_computation.50.clone.1 | convolution fusion | flops 87183680 | bytes 3570048 | tf_op jit(solution)/shard_map/while/body/eval_jaxpr/sub | solution.py:28
  213.1 2.9 %fusion.46 = f32[16,64,129]{2,1,0:T(8,128)S(1)} fusion(bf16[320,16,64]{0,2,1:T(8,128)(2,1)S(1)} %bitcast.74, f32[16,129,320]{2,1,0:T(8,128)} %get-tuple-element.354, f32[16,129]{1,0:T(8,128)S(1)} %get-tuple-element.355), kind=kOutput, calls=%fused_computation.9.clone.1 | convolution fusion | flops 85862400 | bytes 3833920 | tf_op jit(solution)/shard_map/while/body/eval_jaxpr/bhqk,bkhe->bqhe/dot_general | solution.py:30
  228.3 3.0 %fusion.45 = (f32[16,129]{1,0:T(8,128)S(1)}, f32[16,129,320]{2,1,0:T(8,128)}) fusion(pred[320]{0:T(512)(128)(4,1)S(1)} %add_reduce_fusion.2, bf16[129,16,64]{0,2,1:T(8,128)(2,1)S(1)} %bitcast.76, bf16[320,16,64]{0,2,1:T(8,128)(2,1)S(1)} %bitcast.75), kind=kOutput, calls=%fused_computation.50.clone.1 | convolution fusion | flops 87183680 | bytes 3570048 | tf_op jit(solution)/shard_map/while/body/eval_jaxpr/sub | solution.py:28
  231.3 2.9 %fusion.46 = f32[16,64,129]{2,1,0:T(8,128)S(1)} fusion(bf16[320,16,64]{0,2,1:T(8,128)(2,1)S(1)} %bitcast.74, f32[16,129,320]{2,1,0:T(8,128)} %get-tuple-element.354, f32[16,129]{1,0:T(8,128)S(1)} %get-tuple-element.355), kind=kOutput, calls=%fused_computation.9.clone.1 | convolution fusion | flops 85862400 | bytes 3833920 | tf_op jit(solution)/shard_map/while/body/eval_jaxpr/bhqk,bkhe->bqhe/dot_general | solution.py:30
  235.9 3.0 %slice.51 = f32[4,1,128,1024]{2,3,1,0:T(8,128)} slice(f32[4,1,129,1024]{2,3,1,0:T(8,128)} %get-tuple-element.165), slice={[0:4], [0:1], [0:128], [0:1024]} | slice | bytes 4194304 | tf_op jit(solution)/shard_map/slice | solution.py:103
  239.0 3.7 %copy.35 = bf16[4,1,129,1024]{3,0,2,1:T(4,128)(2,1)S(1)} copy(f32[4,1,129,1024]{2,3,1,0:T(8,128)} %get-tuple-element.165) | data formatting | bytes 3170304 | tf_op jit(solution)/shard_map/while | solution.py:101
  242.7 1.9 copy.34
  (114 shorter events, 50.3 us)
Async XLA Ops:
  7.2 49.9 %copy-start.3 = (bf16[1,512,1024]{2,1,0:T(8,128)(2,1)S(1)}, bf16[1,512,1024]{2,1,0:T(8,128)(2,1)}, u32[]{:S(2)}) copy-start(bf16[1,512,1024]{2,1,0:T(8,128)(2,1)} %param.8) | copy-start | bytes 3145732
  7.2 49.9 %all-gather.4.cloned.1.call-start = ((), (), s32[]{:S(2)}) async-start(), calls=%async_computation | async-start | bytes 2621440 | tf_op jit(solution)/shard_map/all_gather | solution.py:65
  7.9 95.2 %all-gather.8.cloned.1.call-start = ((), (), s32[]{:S(2)}) async-start(), calls=%async_computation.2 | async-start | bytes 2621440 | tf_op jit(solution)/shard_map/all_gather | solution.py:64
  8.7 140.5 %all-gather.6.cloned.1.call-start = ((), (), s32[]{:S(2)}) async-start(), calls=%async_computation.1 | async-start | bytes 2621440 | tf_op jit(solution)/shard_map/all_gather | solution.py:63
  61.4 96.5 %collective-permute-start.1 = (bf16[1,32,1024]{2,1,0:T(8,128)(2,1)}, bf16[1,32,1024]{2,1,0:T(8,128)(2,1)S(1)}, u32[]{:S(2)}, u32[]{:S(2)}) collective-permute-start(bf16[1,32,1024]{2,1,0:T(8,128)(2,1)} %get-tuple-element.268), channel_id=1, source_target_pairs={{1,0},{2,1},{3,2},{4,3},{5,4},{6,5},{7,6},{9,8},{10,9},{11,10},{12... | collective-permute-start | bytes 196616 | tf_op jit(solution)/shard_map/ppermute | solution.py:14
  64.0 94.0 %collective-permute-start = (bf16[1,128,1024]{2,1,0:T(8,128)(2,1)}, bf16[1,128,1024]{2,1,0:T(8,128)(2,1)}, u32[]{:S(2)}, u32[]{:S(2)}) collective-permute-start(bf16[1,128,1024]{2,1,0:T(8,128)(2,1)} %slice.53), channel_id=1, source_target_pairs={{0,1},{1,2},{2,3},{3,4},{4,5},{5,6},{6,7},{8,9},{9,10},{10,11},{11... | collective-permute-start | bytes 786440 | tf_op jit(solution)/shard_map/ppermute | solution.py:14
  106.1 47.1 %copy-start.2 = (bf16[1,548,1024]{2,1,0:T(8,128)(2,1)}, bf16[1,548,1024]{2,1,0:T(8,128)(2,1)S(1)}, u32[]{:S(2)}) copy-start(bf16[1,548,1024]{2,1,0:T(8,128)(2,1)S(1)} %fusion.17) | copy-start | bytes 3366916
  106.9 54.0 %collective-permute-start.2 = (bf16[1,128,1024]{2,1,0:T(8,128)(2,1)}, bf16[1,128,1024]{2,1,0:T(8,128)(2,1)}, u32[]{:S(2)}, u32[]{:S(2)}) collective-permute-start(bf16[1,128,1024]{2,1,0:T(8,128)(2,1)} %slice.59), channel_id=1, source_target_pairs={{0,1},{1,2},{2,3},{3,4},{4,5},{5,6},{6,7},{8,9},{9,10},{10,11},{11... | collective-permute-start | bytes 786440 | tf_op jit(solution)/shard_map/ppermute | solution.py:14
  154.2 6.6 %slice-start = ((bf16[1,548,1024]{2,1,0:T(8,128)(2,1)}), bf16[1,512,1024]{2,1,0:T(8,128)(2,1)S(1)}, s32[]{:S(2)}) async-start(bf16[1,548,1024]{2,1,0:T(8,128)(2,1)} %copy-done.2), calls=%async_computation.3 | async-start | bytes 2097152 | tf_op jit(solution)/shard_map/slice | solution.py:73
  154.2 6.6 %collective-permute-start.3 = (bf16[1,32,1024]{2,1,0:T(8,128)(2,1)S(1)}, bf16[1,32,1024]{2,1,0:T(8,128)(2,1)S(1)}, u32[]{:S(2)}, u32[]{:S(2)}) collective-permute-start(bf16[1,32,1024]{2,1,0:T(8,128)(2,1)S(1)} %get-tuple-element.266), channel_id=1, source_target_pairs={{1,0},{2,1},{3,2},{4,3},{5,4},{6,5},{7,6},{9,8},{10,9},{11,10},{12... | collective-permute-start | bytes 196616 | tf_op jit(solution)/shard_map/ppermute | solution.py:14
  163.1 1.8 copy-start
  179.6 1.7 copy-start.1
  181.3 1.8 copy-start
  197.8 1.7 copy-start.1
  199.5 1.8 copy-start
  216.0 1.7 copy-start.1
  217.7 1.8 copy-start
  234.2 1.7 copy-start.1
Sparse Core Ops, SparseCore 0:
  9.5 47.5 all-gather.3
  58.7 44.4 all-gather.7
  104.7 44.4 all-gather.5
where the time goes:
time: 254 us; the launch traced here: 253 us
  waiting for transfers between devices  112 us (44%)
  local copies, waits for them, and re-layouts  37.7 us (15%)
  matrix products  33.9 us (13%)
  other arithmetic  18.3 us (7%)
  between operations  14.5 us (6%)
  loops' own time  13.5 us (5%)
  starting transfers between devices  12.8 us (5%)
  blocking collectives  9.73 us (4%)
    all_gather x1, waiting for transfers between devices, local(): q_flat = project_one(lax.all_gather(w_query, 'dp', axis=1, tiled=True))  38.7 us
    all_gather x1, waiting for transfers between devices, local(): k_flat = project_one(lax.all_gather(w_key, 'dp', axis=1, tiled=True))  35.3 us
    all_gather x1, waiting for transfers between devices, local(): v_flat = project_one(lax.all_gather(w_value, 'dp', axis=1, tiled=True))  34.8 us
    another operation x1, loops' own time, local(): attended = lax.map(one_segment, jnp.arange(seg_dev, dtype=jnp.int32))  13.5 us
    ppermute x4, starting transfers between devices, passed_along(): return lax.ppermute(block, axis, route)  12.7 us
    sub x4, matrix products, attend(): probs = jnp.exp(scores - row_max)  12.1 us
    dot_general x4, matrix products, attend(): jnp.einsum('bhqk,bkhe->bqhe', weights, v_heads, preferred_element_type=jn...  11.6 us
    all_gather x1, blocking collectives, local(): bank_rows = lax.all_gather(memory_in, 'seq', axis=1, tiled=True)  9.73 us
  transfers between devices with their start and end apart: 7, of which 4 were waited for; matrix products, arithmetic and copies ran while one was open for 7% of the time, Pallas kernels for 0%

commit v1 on v0

v1 whole, which is shorter than its diff:
```python
import jax
import jax.numpy as jnp
from jax import lax
from jax.experimental import pallas as pl
from jax.experimental.pallas import tpu as pltpu
from jax.sharding import PartitionSpec as P

HEADS = 16
LEFT = 128
RIGHT = 32
LANES = 128
PAD_ROWS = 16
DEAD = -1e30


def shifted(block, axis, distance):
    count = lax.axis_size(axis)
    route = [(i - distance, i) for i in range(count) if 0 <= i - distance < count]
    return lax.ppermute(block, axis, route)


def swapped(block, axis, masks):
    count = lax.axis_size(axis)
    return lax.ppermute(block, axis, [(i, i ^ masks[i % 2]) for i in range(count)])


def stage_masks(count):
    bits = [1 << b for b in range(1, count.bit_length() - 1)]
    turned = bits[1:] + bits[:1]
    return [pair for pair in zip(bits, turned)] + [(1, 1)]


def gather_slices(mine, axis):
    index = lax.axis_index(axis)
    odd = index % 2
    buffers = [mine[None]]
    owners = [(0, 0)]
    for even_mask, odd_mask in stage_masks(lax.axis_size(axis)):
        sent = buffers[0] if len(buffers) == 1 else jnp.concatenate(buffers, axis=0)
        buffers.append(swapped(sent, axis, (even_mask, odd_mask)))
        if even_mask == 1:
            owners = owners + [(o ^ 1, e ^ 1) for e, o in owners]
        else:
            owners = owners + [(e ^ even_mask, o ^ odd_mask) for e, o in owners]
    slots = [index ^ jnp.where(odd == 1, o, e) for e, o in owners]
    return buffers, slots


def gather_bank(memory_in, axis):
    index = lax.axis_index(axis)
    count = lax.axis_size(axis)
    bank = memory_in
    bit = 1
    while bit < count:
        bank = jnp.concatenate([bank, swapped(bank, axis, (bit, bit))], axis=1)
        bit *= 2
    return bank, index


def make_kernel(dims, first, slot_counts):
    utts, rows, feat, cols, segs, seg_len, bank_n = dims
    hd = feat // HEADS
    per_tile = LANES // hd
    span = LEFT + seg_len + RIGHT
    kv_rows = bank_n + LEFT + rows + RIGHT
    q_base = bank_n + LEFT
    q_rows = rows + RIGHT + PAD_ROWS
    scale = float(hd) ** (-0.5)

    def kernel(*refs):
        refs = list(refs)
        scal_ref = refs.pop(0)
        len_ref = refs.pop(0)
        if first:
            frames_ref, left_ref, right_ref, bank_ref = refs[:4]
            refs = refs[4:]
            w_refs = refs[:3]
            refs = refs[3:]
            ctx_ref, mem_ref, x_ref = refs[:3]
            refs = refs[3:]
        else:
            x_ref = refs.pop(0)
            w_refs = refs[: len(slot_counts)]
            refs = refs[len(slot_counts) + 2 :]
            ctx_ref, mem_ref = refs[:2]
            refs = refs[2:]
        k_scr, v_scr, q_scr, o_scr, m_scr, in_sem, out_sem = refs
        col = scal_ref[0]
        seq_index = scal_ref[1]
        row_base = seq_index * rows

        if first:
            copies = []
            for u in range(utts):
                for n, (src, at, size) in enumerate(
                    (
                        (bank_ref, 0, bank_n),
                        (left_ref, bank_n, LEFT),
                        (frames_ref, q_base, rows),
                        (right_ref, q_base + rows, RIGHT),
                    )
                ):
                    copies.append(
                        pltpu.make_async_copy(
                            src.at[u], x_ref.at[u, pl.ds(at, size)], in_sem.at[u, n]
                        )
                    )
            for c in copies:
                c.start()
            for c in copies:
                c.wait()
            for u in range(utts):
                length = len_ref[u]
                seg_of = lax.broadcasted_iota(jnp.int32, (PAD_ROWS, rows), 0)
                pos = lax.broadcasted_iota(jnp.int32, (PAD_ROWS, rows), 1)
                pick = (pos // seg_len == seg_of) & (row_base + pos < length)
                own = x_ref[u, q_base : q_base + rows, :]
                sums = jnp.dot(
                    jnp.where(pick, 1.0, 0.0).astype(jnp.bfloat16),
                    own,
                    preferred_element_type=jnp.float32,
                )
                seg = lax.broadcasted_iota(jnp.int32, (PAD_ROWS, 1), 0)
                count = jnp.clip(length - (row_base + seg * seg_len), 1, seg_len)
                mean = sums / count.astype(jnp.float32)
                x_ref[u, q_base + rows + RIGHT :, :] = mean.astype(jnp.bfloat16)

        lane = lax.broadcasted_iota(jnp.int32, (1, LANES), 1)
        waits = []
        for u in range(utts):
            length = len_ref[u]

            def project(which, lo, size):
                if first or len(slot_counts) == 1 and slot_counts[0] == 0:
                    w = w_refs[which][...] if first else w_refs[0][which]
                    return jnp.dot(
                        x_ref[u, lo : lo + size, :], w, preferred_element_type=jnp.float32
                    )
                flat = [(b, n) for b, c in enumerate(slot_counts) for n in range(c)]
                per = feat // len(flat)
                acc = None
                for t in range(0, len(flat), 2):
                    lhs = []
                    rhs = []
                    for s in (t, t + 1):
                        b, n = flat[s]
                        at = pl.multiple_of(scal_ref[2 + s] * per, LANES)
                        lhs.append(x_ref[u, lo : lo + size, pl.ds(at, per)])
                        rhs.append(w_refs[b][n, which])
                    part = jnp.dot(
                        jnp.concatenate(lhs, axis=1),
                        jnp.concatenate(rhs, axis=0),
                        preferred_element_type=jnp.float32,
                    )
                    acc = part if acc is None else acc + part
                return acc

            k_scr[u] = project(1, 0, kv_rows).astype(jnp.bfloat16)
            v_scr[u] = project(2, 0, kv_rows).astype(jnp.bfloat16)
            q_scr[u] = project(0, q_base, q_rows).astype(jnp.bfloat16)
            n_key = bank_n + span
            key_at = lax.broadcasted_iota(jnp.int32, (1, n_key), 1)
            per_dev = segs
            owner = seq_index ^ (key_at // per_dev)
            entry = owner * per_dev + key_at % per_dev
            for s in range(segs):
                seg_index = seq_index * segs + s
                pos = row_base + s * seg_len - LEFT + (key_at - bank_n)
                bank_live = (key_at < bank_n) & (entry < seg_index) & (entry * seg_len < length)
                frame_live = (key_at >= bank_n) & (pos >= 0) & (pos < length)
                bias = jnp.where(bank_live | frame_live, 0.0, DEAD)
                row_at = lax.broadcasted_iota(jnp.int32, (seg_len, 1), 0)
                row_live = (row_base + s * seg_len + row_at) < length
                for p in range(cols // LANES):
                    at = p * LANES
                    win = bank_n + s * seg_len
                    kw = jnp.concatenate(
                        [
                            k_scr[u, :bank_n, at : at + LANES],
                            k_scr[u, win : win + span, at : at + LANES],
                        ],
                        axis=0,
                    )
                    vw = jnp.concatenate(
                        [
                            v_scr[u, :bank_n, at : at + LANES],
                            v_scr[u, win : win + span, at : at + LANES],
                        ],
                        axis=0,
                    )
                    q = jnp.concatenate(
                        [
                            q_scr[u, s * seg_len : (s + 1) * seg_len, at : at + LANES],
                            q_scr[u, rows + RIGHT :, at : at + LANES],
                        ],
                        axis=0,
                    )
                    n_q = seg_len + PAD_ROWS
                    zero = jnp.zeros_like(q)
                    heads = [
                        jnp.where((lane >= h * hd) & (lane < (h + 1) * hd), q, zero)
                        for h in range(per_tile)
                    ]
                    scores = lax.dot_general(
                        jnp.concatenate(heads, axis=0),
                        kw,
                        (((1,), (1,)), ((), ())),
                        preferred_element_type=jnp.float32,
                    )
                    scores = scores * scale + bias
                    top = jnp.max(scores, axis=-1, keepdims=True)
                    probs = jnp.exp(scores - top)
                    total = jnp.sum(probs, axis=-1, keepdims=True)
                    mixed = jnp.dot(
                        probs.astype(jnp.bfloat16), vw, preferred_element_type=jnp.float32
                    )
                    mixed = mixed / total
                    out = mixed[:n_q]
                    for h in range(1, per_tile):
                        out = jnp.where(lane >= h * hd, mixed[h * n_q : (h + 1) * n_q], out)
                    live_rows = jnp.where(row_live, out[:seg_len], 0.0)
                    o_scr[u, s * seg_len : (s + 1) * seg_len, at : at + LANES] = live_rows.astype(
                        jnp.bfloat16
                    )
                    m_scr[u, s : s + 1, at : at + LANES] = out[seg_len + s : seg_len + s + 1]
                done = pltpu.make_async_copy(
                    o_scr.at[u, pl.ds(s * seg_len, seg_len)],
                    ctx_ref.at[u, pl.ds(s * seg_len, seg_len), pl.ds(pl.multiple_of(col * cols, LANES), cols)],
                    out_sem.at[u, s],
                )
                done.start()
                waits.append(done)
        mem_ref[...] = m_scr[...].astype(jnp.bfloat16)
        for done in waits:
            done.wait()

    return kernel


def attend_chunk(dims, first, scal, lengths, inputs, weights, previous):
    utts, rows, feat, cols, segs, seg_len, bank_n = dims
    kv_rows = bank_n + LEFT + rows + RIGHT
    q_rows = rows + RIGHT + PAD_ROWS
    x_rows = kv_rows + PAD_ROWS
    slot_counts = () if first else tuple(w.shape[0] for w in weights)
    if not first and weights[0].ndim == 3:
        slot_counts = (0,)
    anywhere = pl.BlockSpec(memory_space=pl.ANY)
    whole = pl.BlockSpec(memory_space=pltpu.VMEM)
    mem_block = pl.BlockSpec((utts, segs, cols), lambda i, s, n: (0, 0, s[0]))
    ctx_shape = jax.ShapeDtypeStruct((utts, rows, feat), jnp.bfloat16)
    mem_shape = jax.ShapeDtypeStruct((utts, segs, feat), jnp.bfloat16)
    if first:
        in_specs = [anywhere] * 4 + [whole] * len(weights)
        args = list(inputs) + list(weights)
        out_specs = [anywhere, mem_block, whole]
        out_shape = [
            ctx_shape,
            mem_shape,
            jax.ShapeDtypeStruct((utts, x_rows, feat), jnp.bfloat16),
        ]
        aliases = {}
    else:
        in_specs = [whole] * (1 + len(weights)) + [anywhere] * 2
        args = list(inputs) + list(weights) + list(previous)
        out_specs = [anywhere, mem_block]
        out_shape = [ctx_shape, mem_shape]
        aliases = {len(args): 0, len(args) + 1: 1}
    return pl.pallas_call(
        make_kernel(dims, first, slot_counts),
        grid_spec=pltpu.PrefetchScalarGridSpec(
            num_scalar_prefetch=2,
            grid=(1,),
            in_specs=in_specs,
            out_specs=out_specs,
            scratch_shapes=[
                pltpu.VMEM((utts, kv_rows, cols), jnp.bfloat16),
                pltpu.VMEM((utts, kv_rows, cols), jnp.bfloat16),
                pltpu.VMEM((utts, q_rows, cols), jnp.bfloat16),
                pltpu.VMEM((utts, rows, cols), jnp.bfloat16),
                pltpu.VMEM((utts, segs, cols), jnp.float32),
                pltpu.SemaphoreType.DMA((utts, 4)),
                pltpu.SemaphoreType.DMA((utts, segs)),
            ],
        ),
        out_shape=out_shape,
        input_output_aliases=aliases,
        compiler_params=pltpu.CompilerParams(vmem_limit_bytes=20 * 1024 * 1024),
        name="attend_first" if first else "attend_next",
    )(scal, lengths, *args)


def local(frames_in, memory_in, w_query, w_key, w_value, lengths):
    utts, rows, feat = frames_in.shape
    segs = memory_in.shape[1]
    seg_len = rows // segs
    seq_count = lax.axis_size("seq")
    dp_count = lax.axis_size("dp")
    seq_index = lax.axis_index("seq")
    dp_index = lax.axis_index("dp")
    bank_n = segs * seq_count
    part = feat // seq_count
    sliced = part % LANES == 0 and w_query.shape[1] % LANES == 0
    cols = w_query.shape[1] if sliced else feat // 4
    dims = (utts, rows, feat, cols, segs, seg_len, bank_n)

    later = []
    if sliced:
        mine = jnp.stack(
            [
                lax.dynamic_slice_in_dim(w, seq_index * part, part, 0)
                for w in (w_query, w_key, w_value)
            ]
        )
        arrived = [
            lax.ppermute(mine, "dp", [(i, i ^ r) for i in range(dp_count)])
            for r in range(1, dp_count)
        ]
        for r in range(1, dp_count):
            buffers, slots = gather_slices(arrived[r - 1], "seq")
            later.append((dp_index ^ r, slots, buffers))
        own = (dp_index, (w_query, w_key, w_value))
    else:
        full = [lax.all_gather(w, "dp", axis=1, tiled=True) for w in (w_query, w_key, w_value)]
        chunks = [
            (c, [w[:, c * cols : (c + 1) * cols] for w in full]) for c in range(feat // cols)
        ]
        own = chunks[0]
        later = [(c, [], [jnp.stack(ws)]) for c, ws in chunks[1:]]

    left = shifted(frames_in[:, rows - LEFT :], "seq", 1)
    right = shifted(frames_in[:, :RIGHT], "seq", -1)
    bank, _ = gather_bank(memory_in, "seq")

    def scalars(source, slots):
        return jnp.stack([jnp.asarray(v, jnp.int32) for v in [source, seq_index] + list(slots)])

    context, memory_out, x_all = attend_chunk(
        dims,
        True,
        scalars(own[0], []),
        lengths,
        (frames_in, left, right, bank),
        own[1],
        (),
    )
    for source, slots, buffers in later:
        context, memory_out = attend_chunk(
            dims, False, scalars(source, slots), lengths, (x_all,), buffers, (context, memory_out)
        )
    return context, memory_out


def solution(mesh):
    placed = (
        P("dp", "seq", None),
        P("dp", "seq", None),
        P(None, "dp"),
        P(None, "dp"),
        P(None, "dp"),
        P("dp"),
    )
    return jax.shard_map(
        local,
        mesh=mesh,
        in_specs=placed,
        out_specs=(P("dp", "seq", None), P("dp", "seq", None)),
        check_vma=False,
    )
```

time: 254 us -> 94 us (0.37)
  waiting for transfers between devices: 112 us -> 27.6 us
  matrix products: 33.9 us -> 0 us
  local copies, waits for them, and re-layouts: 37.7 us -> 5.85 us
  Pallas kernels: 0 us -> 29.1 us
  other arithmetic: 18.3 us -> 3.92 us
  loops' own time: 13.5 us -> 0 us
  between operations: 14.5 us -> 1.43 us
  starting transfers between devices: 12.8 us -> 24.7 us
  blocking collectives: 9.73 us -> 0 us
    all_gather x3 -> x0, waiting for transfers between devices: 109 us -> none  [the longest x1 38.7 us: local(): q_flat = project_one(lax.all_gather(w_query, 'dp', axis=1, tiled=True))]
    pallas_call x0 -> x4, Pallas kernels: none -> 29.1 us  [attend_chunk(): pl.pallas_call(make_kernel(dims, first, slot_counts), grid_spec=pltpu.Pre...]
    ppermute x4 -> x17, waiting for transfers between devices: 1.55 us -> 27.6 us  [the longest x12 12.7 us: swapped(): lax.ppermute(block, axis, [(i, i ^ masks[i % 2]) for i in range(count)])]
    dot_general x8 -> x0, matrix products: 21.9 us -> none  [the longest x4 11.6 us: attend(): jnp.einsum('bhqk,bkhe->bqhe', weights, v_heads, preferred_element_type=jn...]
    dynamic_slice x36 -> x0, local copies, waits for them, and re-layouts: 15.6 us -> none  [the longest x8 5.85 us: one_segment(): k_window = lax.dynamic_slice_in_dim(k_ext, seg_index * seg_len, key_span, 1)]
    another operation x1 -> x0, loops' own time: 13.5 us -> none  [local(): attended = lax.map(one_segment, jnp.arange(seg_dev, dtype=jnp.int32))]
    sub x4 -> x0, matrix products: 12.1 us -> none  [attend(): probs = jnp.exp(scores - row_max)]
    ppermute x4 -> x17, starting transfers between devices: 12.7 us -> 24.7 us  [the longest x12 14.5 us: swapped(): lax.ppermute(block, axis, [(i, i ^ masks[i % 2]) for i in range(count)])]
  transfers between devices with their start and end apart: 7 -> 17, of which waited for: 4 -> 8; matrix products, arithmetic and copies ran while one was open for 7% -> 5% of each run, Pallas kernels for 0% -> 24%
where the time goes in v1:
time: 94 us; the launch traced here: 92.6 us
  Pallas kernels  29.1 us (31%)
  waiting for transfers between devices  27.6 us (29%)
  starting transfers between devices  24.7 us (26%)
  local copies, waits for them, and re-layouts  5.85 us (6%)
  other arithmetic  3.92 us (4%)
  between operations  1.43 us (2%)
    pallas_call x4, Pallas kernels, attend_chunk(): pl.pallas_call(make_kernel(dims, first, slot_counts), grid_spec=pltpu.Pre...  29.1 us
    ppermute x12, starting transfers between devices, swapped(): lax.ppermute(block, axis, [(i, i ^ masks[i % 2]) for i in range(count)])  14.5 us
    ppermute x12, waiting for transfers between devices, swapped(): lax.ppermute(block, axis, [(i, i ^ masks[i % 2]) for i in range(count)])  12.7 us
    ppermute x3, waiting for transfers between devices, local(): lax.ppermute(mine, 'dp', [(i, i ^ r) for i in range(dp_count)])  11.2 us
    ppermute x2, starting transfers between devices, shifted(): return lax.ppermute(block, axis, route)  6.51 us
    ppermute x2, waiting for transfers between devices, shifted(): return lax.ppermute(block, axis, route)  3.78 us
    ppermute x3, starting transfers between devices, local(): lax.ppermute(mine, 'dp', [(i, i ^ r) for i in range(dp_count)])  3.67 us
    unnamed x10, local copies, waits for them, and re-layouts  3.13 us
  transfers between devices with their start and end apart: 17, of which 8 were waited for; matrix products, arithmetic and copies ran while one was open for 5% of the time, Pallas kernels for 24%

profile of v1, /device:TPU:3, one launch (start us, length us, event | category | flops | bytes accessed | tf_op | source)
XLA Modules:
  0.0 92.6 jit_solution(12959350397660708798)
XLA Ops:
  2.4 1.4 %collective-permute-start.13 = (bf16[3,128,256]{2,1,0:T(8,128)(2,1)S(1)}, bf16[3,128,256]{2,1,0:T(8,128)(2,1)S(1)}, u32[]{:S(2)}, u32[]{:S(2)}) collective-permute-start(bf16[3,128,256]{2,1,0:T(8,128)(2,1)S(1)} %pad_maximum_fusion.6), channel_id=1, source_target_pairs={{0,8},{8,0},{16,24},{24,16},{1,9},{9,1},{17,25},{25,17},{2,10},{10... | collective-permute-start | bytes 589832 | tf_op jit(solution)/shard_map/ppermute | solution.py:316
  3.8 2.3 %collective-permute-start.9 = (bf16[3,128,256]{2,1,0:T(8,128)(2,1)S(1)}, bf16[3,128,256]{2,1,0:T(8,128)(2,1)S(1)}, u32[]{:S(2)}, u32[]{:S(2)}) collective-permute-start(bf16[3,128,256]{2,1,0:T(8,128)(2,1)S(1)} %pad_maximum_fusion.6), channel_id=1, source_target_pairs={{0,16},{8,24},{16,0},{24,8},{1,17},{9,25},{17,1},{25,9},{2,18},{10... | collective-permute-start | bytes 589832 | tf_op jit(solution)/shard_map/ppermute | solution.py:316
  6.1 5.3 %collective-permute-done.13 = bf16[3,128,256]{2,1,0:T(8,128)(2,1)S(1)} collective-permute-done((bf16[3,128,256]{2,1,0:T(8,128)(2,1)S(1)}, bf16[3,128,256]{2,1,0:T(8,128)(2,1)S(1)}, u32[]{:S(2)}, u32[]{:S(2)}) %collective-permute-start.13) | collective-permute-done | bytes 196640 | tf_op jit(solution)/shard_map/ppermute | solution.py:316
  11.4 1.2 %collective-permute-start.14 = (bf16[1,3,128,256]{3,2,1,0:T(8,128)(2,1)S(1)}, bf16[1,3,128,256]{3,2,1,0:T(8,128)(2,1)S(1)}, u32[]{:S(2)}, u32[]{:S(2)}) collective-permute-start(bf16[1,3,128,256]{3,2,1,0:T(8,128)(2,1)S(1)} %bitcast.29), channel_id=1, source_target_pairs={{0,2},{1,5},{2,0},{3,7},{4,6},{5,1},{6,4},{7,3},{8,10},{9,13},{10,... | collective-permute-start | bytes 589832 | tf_op jit(solution)/shard_map/ppermute | solution.py:24
  12.8 5.9 %collective-permute-done.5 = bf16[3,128,256]{2,1,0:T(8,128)(2,1)S(1)} collective-permute-done((bf16[3,128,256]{2,1,0:T(8,128)(2,1)S(1)}, bf16[3,128,256]{2,1,0:T(8,128)(2,1)S(1)}, u32[]{:S(2)}, u32[]{:S(2)}) %collective-permute-start.5) | collective-permute-done | bytes 196640 | tf_op jit(solution)/shard_map/ppermute | solution.py:316
  18.8 1.2 %collective-permute-start.6 = (bf16[1,3,128,256]{3,2,1,0:T(8,128)(2,1)S(1)}, bf16[1,3,128,256]{3,2,1,0:T(8,128)(2,1)S(1)}, u32[]{:S(2)}, u32[]{:S(2)}) collective-permute-start(bf16[1,3,128,256]{3,2,1,0:T(8,128)(2,1)S(1)} %bitcast.21), channel_id=1, source_target_pairs={{0,2},{1,5},{2,0},{3,7},{4,6},{5,1},{6,4},{7,3},{8,10},{9,13},{10,... | collective-permute-start | bytes 589832 | tf_op jit(solution)/shard_map/ppermute | solution.py:24
  20.4 1.3 %collective-permute-start.11 = (bf16[2,3,128,256]{3,2,1,0:T(8,128)(2,1)S(1)}, bf16[2,3,128,256]{3,2,1,0:T(8,128)(2,1)S(1)}, u32[]{:S(2)}, u32[]{:S(2)}) collective-permute-start(bf16[2,3,128,256]{3,2,1,0:T(8,128)(2,1)S(1)} %pad_maximum_fusion.4), channel_id=1, source_target_pairs={{0,4},{1,3},{2,6},{3,1},{4,0},{5,7},{6,2},{7,5},{8,12},{9,11},{10,... | collective-permute-start | bytes 1179656 | tf_op jit(solution)/shard_map/ppermute | solution.py:24
  21.7 1.6 %collective-permute-done.6.refs_4_ = bf16[1,3,128,256]{3,2,1,0:T(8,128)(2,1)S(1)} collective-permute-done((bf16[1,3,128,256]{3,2,1,0:T(8,128)(2,1)S(1)}, bf16[1,3,128,256]{3,2,1,0:T(8,128)(2,1)S(1)}, u32[]{:S(2)}, u32[]{:S(2)}) %collective-permute-start.6) | collective-permute-done | bytes 196640 | tf_op jit(solution)/shard_map/ppermute | solution.py:24
  23.6 5.4 %collective-permute-done.15.refs_5_ = bf16[2,3,128,256]{3,2,1,0:T(8,128)(2,1)S(1)} collective-permute-done((bf16[2,3,128,256]{3,2,1,0:T(8,128)(2,1)S(1)}, bf16[2,3,128,256]{3,2,1,0:T(8,128)(2,1)S(1)}, u32[]{:S(2)}, u32[]{:S(2)}) %collective-permute-start.15) | collective-permute-done | bytes 393248 | tf_op jit(solution)/shard_map/ppermute | solution.py:24
  30.0 6.4 %collective-permute-start.16 = (bf16[4,3,128,256]{3,2,1,0:T(8,128)(2,1)}, bf16[4,3,128,256]{3,2,1,0:T(8,128)(2,1)}, u32[]{:S(2)}, u32[]{:S(2)}) collective-permute-start(bf16[4,3,128,256]{3,2,1,0:T(8,128)(2,1)} %pad_maximum_fusion.2), channel_id=1, source_target_pairs={{0,1},{1,0},{2,3},{3,2},{4,5},{5,4},{6,7},{7,6},{8,9},{9,8},{10,11... | collective-permute-start | bytes 2359304 | tf_op jit(solution)/shard_map/ppermute | solution.py:24
  37.4 1.1 %collective-permute-start.12 = (bf16[4,3,128,256]{3,2,1,0:T(8,128)(2,1)}, bf16[4,3,128,256]{3,2,1,0:T(8,128)(2,1)}, u32[]{:S(2)}, u32[]{:S(2)}) collective-permute-start(bf16[4,3,128,256]{3,2,1,0:T(8,128)(2,1)} %pad_maximum_fusion.1), channel_id=1, source_target_pairs={{0,1},{1,0},{2,3},{3,2},{4,5},{5,4},{6,7},{7,6},{8,9},{9,8},{10,11... | collective-permute-start | bytes 2359304 | tf_op jit(solution)/shard_map/ppermute | solution.py:24
  38.4 1.2 %collective-permute-done.7.refs_5_ = bf16[2,3,128,256]{3,2,1,0:T(8,128)(2,1)S(1)} collective-permute-done((bf16[2,3,128,256]{3,2,1,0:T(8,128)(2,1)S(1)}, bf16[2,3,128,256]{3,2,1,0:T(8,128)(2,1)S(1)}, u32[]{:S(2)}, u32[]{:S(2)}) %collective-permute-start.7) | collective-permute-done | bytes 393248 | tf_op jit(solution)/shard_map/ppermute | solution.py:24
  40.6 2.0 %collective-permute-start.8 = (bf16[4,3,128,256]{3,2,1,0:T(8,128)(2,1)}, bf16[4,3,128,256]{3,2,1,0:T(8,128)(2,1)}, u32[]{:S(2)}, u32[]{:S(2)}) collective-permute-start(bf16[4,3,128,256]{3,2,1,0:T(8,128)(2,1)} %pad_maximum_fusion), channel_id=1, source_target_pairs={{0,1},{1,0},{2,3},{3,2},{4,5},{5,4},{6,7},{7,6},{8,9},{9,8},{10,11... | collective-permute-start | bytes 2359304 | tf_op jit(solution)/shard_map/ppermute | solution.py:24
  42.7 2.2 %collective-permute-done.2 = bf16[1,4,1024]{2,1,0:T(4,128)(2,1)S(1)} collective-permute-done((bf16[1,4,1024]{2,1,0:T(4,128)(2,1)S(1)}, bf16[1,4,1024]{2,1,0:T(4,128)(2,1)S(1)}, u32[]{:S(2)}, u32[]{:S(2)}) %collective-permute-start.2) | collective-permute-done | bytes 8224 | tf_op jit(solution)/shard_map/ppermute | solution.py:24
  46.0 4.6 %collective-permute-start = (bf16[1,128,1024]{2,1,0:T(8,128)(2,1)}, bf16[1,128,1024]{2,1,0:T(8,128)(2,1)}, u32[]{:S(2)}, u32[]{:S(2)}) collective-permute-start(bf16[1,128,1024]{2,1,0:T(8,128)(2,1)} %slice.6), channel_id=1, source_target_pairs={{0,1},{1,2},{2,3},{3,4},{4,5},{5,6},{6,7},{8,9},{9,10},{10,11},{11... | collective-permute-start | bytes 786440 | tf_op jit(solution)/shard_map/ppermute | solution.py:19
  51.7 2.2 %collective-permute-done.4 = bf16[1,16,1024]{2,1,0:T(8,128)(2,1)} collective-permute-done((bf16[1,16,1024]{2,1,0:T(8,128)(2,1)S(1)}, bf16[1,16,1024]{2,1,0:T(8,128)(2,1)}, u32[]{:S(2)}, u32[]{:S(2)}) %collective-permute-start.4) | collective-permute-done | bytes 32800 | tf_op jit(solution)/shard_map/ppermute | solution.py:24
  53.8 1.9 %collective-permute-start.1 = (bf16[1,32,1024]{2,1,0:T(8,128)(2,1)S(1)}, bf16[1,32,1024]{2,1,0:T(8,128)(2,1)S(1)}, u32[]{:S(2)}, u32[]{:S(2)}) collective-permute-start(bf16[1,32,1024]{2,1,0:T(8,128)(2,1)S(1)} %slice.7), channel_id=1, source_target_pairs={{1,0},{2,1},{3,2},{4,3},{5,4},{6,5},{7,6},{9,8},{10,9},{11,10},{12... | collective-permute-start | bytes 196616 | tf_op jit(solution)/shard_map/ppermute | solution.py:19
  56.5 3.8 %collective-permute-done.1.refs_4_ = bf16[1,32,1024]{2,1,0:T(8,128)(2,1)S(1)} collective-permute-done((bf16[1,32,1024]{2,1,0:T(8,128)(2,1)S(1)}, bf16[1,32,1024]{2,1,0:T(8,128)(2,1)S(1)}, u32[]{:S(2)}, u32[]{:S(2)}) %collective-permute-start.1) | collective-permute-done | bytes 65568 | tf_op jit(solution)/shard_map/ppermute | solution.py:19
  60.3 1.0 %copy-done.1 = bf16[1024,256]{1,0:T(8,128)(2,1)S(1)} copy-done((bf16[1024,256]{1,0:T(8,128)(2,1)S(1)}, bf16[1024,256]{1,0:T(8,128)(2,1)}, u32[]{:S(2)}) %copy-start.1) | copy-done | bytes 524312
  61.4 1.0 %copy-done.2 = bf16[1024,256]{1,0:T(8,128)(2,1)S(1)} copy-done((bf16[1024,256]{1,0:T(8,128)(2,1)S(1)}, bf16[1024,256]{1,0:T(8,128)(2,1)}, u32[]{:S(2)}) %copy-start.2) | copy-done | bytes 524312
  63.4 7.3 %attend_first.1 = (bf16[1,512,1024]{2,1,0:T(8,128)(2,1)}, bf16[1,4,1024]{2,1,0:T(4,128)(2,1)}, bf16[1,720,1024]{2,1,0:T(8,128)(2,1)S(1)}) custom-call(s32[2]{0:T(128)S(1)} %pad_add_fusion.refs_0_, s32[1]{0:T(128)S(6)} %copy.20.refs_1_, bf16[1,512,1024]{2,1,0:T(8,128)(2,1)S(1)} %copy-done, bf16[1,128,1024]{2,1,0:T(8,128)(2,1)} %collective-permute-done.refs_3_, ...), custom_call_target="tpu_custom_call" | custom-call | tf_op jit(solution)/shard_map/attend_first/pallas_call | solution.py:269
  70.8 7.3 %attend_next.3 = (bf16[1,512,1024]{2,1,0:T(8,128)(2,1)}, bf16[1,4,1024]{2,1,0:T(4,128)(2,1)}) custom-call(s32[10]{0:T(128)S(1)} %stack.99.refs_0_, s32[1]{0:T(128)S(6)} %copy.20.refs_1_, bf16[1,720,1024]{2,1,0:T(8,128)(2,1)S(1)} %get-tuple-element.9.refs_2_, bf16[1,3,128,256]{3,2,1,0:T(8,128)(2,1)S(1)} %bitcast.32, ...), custom_call_target="tpu_custom_call", output_to_operand_aliasing={{0}: (7, {}), {1}: (8, {})} | custom-call | tf_op jit(solution)/shard_map/attend_next/pallas_call | solution.py:269
  78.1 7.3 %attend_next.4 = (bf16[1,512,1024]{2,1,0:T(8,128)(2,1)}, bf16[1,4,1024]{2,1,0:T(4,128)(2,1)}) custom-call(s32[10]{0:T(128)S(1)} %stack.97.refs_0_, s32[1]{0:T(128)S(6)} %copy.20.refs_1_, bf16[1,720,1024]{2,1,0:T(8,128)(2,1)S(1)} %get-tuple-element.9.refs_2_, bf16[1,3,128,256]{3,2,1,0:T(8,128)(2,1)S(1)} %bitcast.28, ...), custom_call_target="tpu_custom_call", output_to_operand_aliasing={{0}: (7, {}), {1}: (8, {})} | custom-call | tf_op jit(solution)/shard_map/attend_next/pallas_call | solution.py:269
  85.4 7.3 %attend_next.5 = (bf16[1,512,1024]{2,1,0:T(8,128)(2,1)}, bf16[1,4,1024]{2,1,0:T(4,128)(2,1)}) custom-call(s32[10]{0:T(128)S(1)} %stack.89.refs_0_, s32[1]{0:T(128)S(6)} %copy.20.refs_1_, bf16[1,720,1024]{2,1,0:T(8,128)(2,1)S(1)} %get-tuple-element.9.refs_2_, bf16[1,3,128,256]{3,2,1,0:T(8,128)(2,1)S(1)} %bitcast.24, ...), custom_call_target="tpu_custom_call", output_to_operand_aliasing={{0}: (7, {}), {1}: (8, {})} | custom-call | tf_op jit(solution)/shard_map/attend_next/pallas_call | solution.py:269
  (42 shorter events, 9.0 us)
Async XLA Ops:
  2.4 9.0 %collective-permute-start.13 = (bf16[3,128,256]{2,1,0:T(8,128)(2,1)S(1)}, bf16[3,128,256]{2,1,0:T(8,128)(2,1)S(1)}, u32[]{:S(2)}, u32[]{:S(2)}) collective-permute-start(bf16[3,128,256]{2,1,0:T(8,128)(2,1)S(1)} %pad_maximum_fusion.6), channel_id=1, source_target_pairs={{0,8},{8,0},{16,24},{24,16},{1,9},{9,1},{17,25},{25,17},{2,10},{10... | collective-permute-start | bytes 589832 | tf_op jit(solution)/shard_map/ppermute | solution.py:316
  3.8 8.9 %collective-permute-start.9 = (bf16[3,128,256]{2,1,0:T(8,128)(2,1)S(1)}, bf16[3,128,256]{2,1,0:T(8,128)(2,1)S(1)}, u32[]{:S(2)}, u32[]{:S(2)}) collective-permute-start(bf16[3,128,256]{2,1,0:T(8,128)(2,1)S(1)} %pad_maximum_fusion.6), channel_id=1, source_target_pairs={{0,16},{8,24},{16,0},{24,8},{1,17},{9,25},{17,1},{25,9},{2,18},{10... | collective-permute-start | bytes 589832 | tf_op jit(solution)/shard_map/ppermute | solution.py:316
  6.1 12.7 %collective-permute-start.5 = (bf16[3,128,256]{2,1,0:T(8,128)(2,1)S(1)}, bf16[3,128,256]{2,1,0:T(8,128)(2,1)S(1)}, u32[]{:S(2)}, u32[]{:S(2)}) collective-permute-start(bf16[3,128,256]{2,1,0:T(8,128)(2,1)S(1)} %pad_maximum_fusion.6), channel_id=1, source_target_pairs={{0,24},{8,16},{16,8},{24,0},{1,25},{9,17},{17,9},{25,1},{2,26},{10... | collective-permute-start | bytes 589832 | tf_op jit(solution)/shard_map/ppermute | solution.py:316
  11.4 8.6 %collective-permute-start.14 = (bf16[1,3,128,256]{3,2,1,0:T(8,128)(2,1)S(1)}, bf16[1,3,128,256]{3,2,1,0:T(8,128)(2,1)S(1)}, u32[]{:S(2)}, u32[]{:S(2)}) collective-permute-start(bf16[1,3,128,256]{3,2,1,0:T(8,128)(2,1)S(1)} %bitcast.29), channel_id=1, source_target_pairs={{0,2},{1,5},{2,0},{3,7},{4,6},{5,1},{6,4},{7,3},{8,10},{9,13},{10,... | collective-permute-start | bytes 589832 | tf_op jit(solution)/shard_map/ppermute | solution.py:24
  12.6 7.7 %collective-permute-start.10 = (bf16[1,3,128,256]{3,2,1,0:T(8,128)(2,1)S(1)}, bf16[1,3,128,256]{3,2,1,0:T(8,128)(2,1)S(1)}, u32[]{:S(2)}, u32[]{:S(2)}) collective-permute-start(bf16[1,3,128,256]{3,2,1,0:T(8,128)(2,1)S(1)} %bitcast.25), channel_id=1, source_target_pairs={{0,2},{1,5},{2,0},{3,7},{4,6},{5,1},{6,4},{7,3},{8,10},{9,13},{10,... | collective-permute-start | bytes 589832 | tf_op jit(solution)/shard_map/ppermute | solution.py:24
  18.8 4.5 %collective-permute-start.6 = (bf16[1,3,128,256]{3,2,1,0:T(8,128)(2,1)S(1)}, bf16[1,3,128,256]{3,2,1,0:T(8,128)(2,1)S(1)}, u32[]{:S(2)}, u32[]{:S(2)}) collective-permute-start(bf16[1,3,128,256]{3,2,1,0:T(8,128)(2,1)S(1)} %bitcast.21), channel_id=1, source_target_pairs={{0,2},{1,5},{2,0},{3,7},{4,6},{5,1},{6,4},{7,3},{8,10},{9,13},{10,... | collective-permute-start | bytes 589832 | tf_op jit(solution)/shard_map/ppermute | solution.py:24
  20.0 9.0 %collective-permute-start.15 = (bf16[2,3,128,256]{3,2,1,0:T(8,128)(2,1)S(1)}, bf16[2,3,128,256]{3,2,1,0:T(8,128)(2,1)S(1)}, u32[]{:S(2)}, u32[]{:S(2)}) collective-permute-start(bf16[2,3,128,256]{3,2,1,0:T(8,128)(2,1)S(1)} %pad_maximum_fusion.5), channel_id=1, source_target_pairs={{0,4},{1,3},{2,6},{3,1},{4,0},{5,7},{6,2},{7,5},{8,12},{9,11},{10,... | collective-permute-start | bytes 1179656 | tf_op jit(solution)/shard_map/ppermute | solution.py:24
  20.4 16.0 %collective-permute-start.11 = (bf16[2,3,128,256]{3,2,1,0:T(8,128)(2,1)S(1)}, bf16[2,3,128,256]{3,2,1,0:T(8,128)(2,1)S(1)}, u32[]{:S(2)}, u32[]{:S(2)}) collective-permute-start(bf16[2,3,128,256]{3,2,1,0:T(8,128)(2,1)S(1)} %pad_maximum_fusion.4), channel_id=1, source_target_pairs={{0,4},{1,3},{2,6},{3,1},{4,0},{5,7},{6,2},{7,5},{8,12},{9,11},{10,... | collective-permute-start | bytes 1179656 | tf_op jit(solution)/shard_map/ppermute | solution.py:24
  23.3 16.3 %collective-permute-start.7 = (bf16[2,3,128,256]{3,2,1,0:T(8,128)(2,1)S(1)}, bf16[2,3,128,256]{3,2,1,0:T(8,128)(2,1)S(1)}, u32[]{:S(2)}, u32[]{:S(2)}) collective-permute-start(bf16[2,3,128,256]{3,2,1,0:T(8,128)(2,1)S(1)} %pad_maximum_fusion.3), channel_id=1, source_target_pairs={{0,4},{1,3},{2,6},{3,1},{4,0},{5,7},{6,2},{7,5},{8,12},{9,11},{10,... | collective-permute-start | bytes 1179656 | tf_op jit(solution)/shard_map/ppermute | solution.py:24
  30.0 12.6 %copy-start.4 = (bf16[1,4,1024]{2,1,0:T(4,128)(2,1)S(1)}, bf16[1,4,1024]{2,1,0:T(4,128)(2,1)}, u32[]{:S(2)}) copy-start(bf16[1,4,1024]{2,1,0:T(4,128)(2,1)} %param.7) | copy-start | bytes 24580
  30.0 15.2 %copy-start = (bf16[1,512,1024]{2,1,0:T(8,128)(2,1)S(1)}, bf16[1,512,1024]{2,1,0:T(8,128)(2,1)}, u32[]{:S(2)}) copy-start(bf16[1,512,1024]{2,1,0:T(8,128)(2,1)} %refs_2_.1) | copy-start | bytes 3145732
  30.0 40.7 %collective-permute-start.16 = (bf16[4,3,128,256]{3,2,1,0:T(8,128)(2,1)}, bf16[4,3,128,256]{3,2,1,0:T(8,128)(2,1)}, u32[]{:S(2)}, u32[]{:S(2)}) collective-permute-start(bf16[4,3,128,256]{3,2,1,0:T(8,128)(2,1)} %pad_maximum_fusion.2), channel_id=1, source_target_pairs={{0,1},{1,0},{2,3},{3,2},{4,5},{5,4},{6,7},{7,6},{8,9},{9,8},{10,11... | collective-permute-start | bytes 2359304 | tf_op jit(solution)/shard_map/ppermute | solution.py:24
  37.4 40.7 %collective-permute-start.12 = (bf16[4,3,128,256]{3,2,1,0:T(8,128)(2,1)}, bf16[4,3,128,256]{3,2,1,0:T(8,128)(2,1)}, u32[]{:S(2)}, u32[]{:S(2)}) collective-permute-start(bf16[4,3,128,256]{3,2,1,0:T(8,128)(2,1)} %pad_maximum_fusion.1), channel_id=1, source_target_pairs={{0,1},{1,0},{2,3},{3,2},{4,5},{5,4},{6,7},{7,6},{8,9},{9,8},{10,11... | collective-permute-start | bytes 2359304 | tf_op jit(solution)/shard_map/ppermute | solution.py:24
  40.6 44.7 %collective-permute-start.8 = (bf16[4,3,128,256]{3,2,1,0:T(8,128)(2,1)}, bf16[4,3,128,256]{3,2,1,0:T(8,128)(2,1)}, u32[]{:S(2)}, u32[]{:S(2)}) collective-permute-start(bf16[4,3,128,256]{3,2,1,0:T(8,128)(2,1)} %pad_maximum_fusion), channel_id=1, source_target_pairs={{0,1},{1,0},{2,3},{3,2},{4,5},{5,4},{6,7},{7,6},{8,9},{9,8},{10,11... | collective-permute-start | bytes 2359304 | tf_op jit(solution)/shard_map/ppermute | solution.py:24
  42.6 2.3 %collective-permute-start.2 = (bf16[1,4,1024]{2,1,0:T(4,128)(2,1)S(1)}, bf16[1,4,1024]{2,1,0:T(4,128)(2,1)S(1)}, u32[]{:S(2)}, u32[]{:S(2)}) collective-permute-start(bf16[1,4,1024]{2,1,0:T(4,128)(2,1)S(1)} %copy-done.4), channel_id=1, source_target_pairs={{0,1},{1,0},{2,3},{3,2},{4,5},{5,4},{6,7},{7,6},{8,9},{9,8},{10,11... | collective-permute-start | bytes 24584 | tf_op jit(solution)/shard_map/ppermute | solution.py:24
  44.9 5.7 %collective-permute-start.3 = (bf16[1,8,1024]{2,1,0:T(8,128)(2,1)S(1)}, bf16[1,8,1024]{2,1,0:T(8,128)(2,1)S(1)}, u32[]{:S(2)}, u32[]{:S(2)}) collective-permute-start(bf16[1,8,1024]{2,1,0:T(8,128)(2,1)S(1)} %pad_maximum_fusion.9), channel_id=1, source_target_pairs={{0,2},{1,3},{2,0},{3,1},{4,6},{5,7},{6,4},{7,5},{8,10},{9,11},{10,... | collective-permute-start | bytes 49160 | tf_op jit(solution)/shard_map/ppermute | solution.py:24
  46.0 14.4 %collective-permute-start = (bf16[1,128,1024]{2,1,0:T(8,128)(2,1)}, bf16[1,128,1024]{2,1,0:T(8,128)(2,1)}, u32[]{:S(2)}, u32[]{:S(2)}) collective-permute-start(bf16[1,128,1024]{2,1,0:T(8,128)(2,1)} %slice.6), channel_id=1, source_target_pairs={{0,1},{1,2},{2,3},{3,4},{4,5},{5,6},{6,7},{8,9},{9,10},{10,11},{11... | collective-permute-start | bytes 786440 | tf_op jit(solution)/shard_map/ppermute | solution.py:19
  50.6 3.2 %collective-permute-start.4 = (bf16[1,16,1024]{2,1,0:T(8,128)(2,1)S(1)}, bf16[1,16,1024]{2,1,0:T(8,128)(2,1)}, u32[]{:S(2)}, u32[]{:S(2)}) collective-permute-start(bf16[1,16,1024]{2,1,0:T(8,128)(2,1)S(1)} %pad_maximum_fusion.8), channel_id=1, source_target_pairs={{0,4},{1,5},{2,6},{3,7},{4,0},{5,1},{6,2},{7,3},{8,12},{9,13},{10,... | collective-permute-start | bytes 98312 | tf_op jit(solution)/shard_map/ppermute | solution.py:24
  53.8 6.5 %collective-permute-start.1 = (bf16[1,32,1024]{2,1,0:T(8,128)(2,1)S(1)}, bf16[1,32,1024]{2,1,0:T(8,128)(2,1)S(1)}, u32[]{:S(2)}, u32[]{:S(2)}) collective-permute-start(bf16[1,32,1024]{2,1,0:T(8,128)(2,1)S(1)} %slice.7), channel_id=1, source_target_pairs={{1,0},{2,1},{3,2},{4,3},{5,4},{6,5},{7,6},{9,8},{10,9},{11,10},{12... | collective-permute-start | bytes 196616 | tf_op jit(solution)/shard_map/ppermute | solution.py:19
  60.3 1.0 %copy-start.1 = (bf16[1024,256]{1,0:T(8,128)(2,1)S(1)}, bf16[1024,256]{1,0:T(8,128)(2,1)}, u32[]{:S(2)}) copy-start(bf16[1024,256]{1,0:T(8,128)(2,1)} %refs_6_.1) | copy-start | bytes 1572868
  61.4 1.0 %copy-start.2 = (bf16[1024,256]{1,0:T(8,128)(2,1)S(1)}, bf16[1024,256]{1,0:T(8,128)(2,1)}, u32[]{:S(2)}) copy-start(bf16[1024,256]{1,0:T(8,128)(2,1)} %refs_7_.1) | copy-start | bytes 1572868
  62.4 1.0 %copy-start.3 = (bf16[1024,256]{1,0:T(8,128)(2,1)S(1)}, bf16[1024,256]{1,0:T(8,128)(2,1)}, u32[]{:S(2)}) copy-start(bf16[1024,256]{1,0:T(8,128)(2,1)} %refs_8_.1) | copy-start | bytes 1572868

commit v2 on v1

--- a/solution.py
+++ b/solution.py
@@ -5,12 +5,14 @@
 from jax.experimental.pallas import tpu as pltpu
 from jax.sharding import PartitionSpec as P
 
+
 HEADS = 16
 LEFT = 128
 RIGHT = 32
 LANES = 128
 PAD_ROWS = 16
 DEAD = -1e30
+MIB = 1024 * 1024
 
 
 def shifted(block, axis, distance):
@@ -32,29 +34,73 @@
 
 def gather_slices(mine, axis):
     index = lax.axis_index(axis)
-    odd = index % 2
-    buffers = [mine[None]]
-    owners = [(0, 0)]
+    blocks = [(mine[None], [(0, 0)])]
     for even_mask, odd_mask in stage_masks(lax.axis_size(axis)):
-        sent = buffers[0] if len(buffers) == 1 else jnp.concatenate(buffers, axis=0)
-        buffers.append(swapped(sent, axis, (even_mask, odd_mask)))
         if even_mask == 1:
-            owners = owners + [(o ^ 1, e ^ 1) for e, o in owners]
-        else:
-            owners = owners + [(e ^ even_mask, o ^ odd_mask) for e, o in owners]
-    slots = [index ^ jnp.where(odd == 1, o, e) for e, o in owners]
-    return buffers, slots
+            for block, owners in list(blocks):
+                got = swapped(block, axis, (1, 1))
+                blocks.append((got, [(o ^ 1, e ^ 1) for e, o in owners]))
+            break
+        owners = [pair for block in blocks for pair in block[1]]
+        sent = blocks[0][0]
+        if len(blocks) > 1:
+            sent = jnp.concatenate([block[0] for block in blocks], axis=0)
+        got = swapped(sent, axis, (even_mask, odd_mask))
+        blocks = [(sent, owners), (got, [(e ^ even_mask, o ^ odd_mask) for e, o in owners])]
+    odd = index % 2 == 1
+    slots = [index ^ jnp.where(odd, o, e) for block in blocks for e, o in block[1]]
+    return [block[0] for block in blocks], slots
 
 
 def gather_bank(memory_in, axis):
-    index = lax.axis_index(axis)
     count = lax.axis_size(axis)
     bank = memory_in
     bit = 1
     while bit < count:
         bank = jnp.concatenate([bank, swapped(bank, axis, (bit, bit))], axis=1)
         bit *= 2
-    return bank, index
+    return bank
+
+
+def cut(seq_index, part, frames_in, weights):
+    utts, rows, feat = frames_in.shape
+    cols = weights[0].shape[1]
+
+    def kernel(scal_ref, f_ref, *refs):
+        w_refs = refs[:3]
+        u_ref, last_ref, head_ref, sem = refs[3:]
+        at = pl.multiple_of(scal_ref[0] * part, part)
+        copies = [
+            pltpu.make_async_copy(w.at[pl.ds(at, part)], u_ref.at[n], sem.at[n])
+            for n, w in enumerate(w_refs)
+        ]
+        copies.append(
+            pltpu.make_async_copy(f_ref.at[:, pl.ds(rows - LEFT, LEFT)], last_ref, sem.at[3])
+        )
+        copies.append(pltpu.make_async_copy(f_ref.at[:, pl.ds(0, RIGHT)], head_ref, sem.at[4]))
+        for c in copies:
+            c.start()
+        for c in copies:
+            c.wait()
+
+    hbm = pl.BlockSpec(memory_space=pltpu.HBM)
+    local = pl.BlockSpec(memory_space=pltpu.VMEM)
+    return pl.pallas_call(
+        kernel,
+        in_specs=[pl.BlockSpec(memory_space=pltpu.SMEM)] + [hbm] * 4,
+        out_specs=[local] * 3,
+        out_shape=[
+            jax.ShapeDtypeStruct((3, part, cols), jnp.bfloat16),
+            jax.ShapeDtypeStruct((utts, LEFT, feat), jnp.bfloat16),
+            jax.ShapeDtypeStruct((utts, RIGHT, feat), jnp.bfloat16),
+        ],
+        scratch_shapes=[pltpu.SemaphoreType.DMA((5,))],
+        compiler_params=pltpu.CompilerParams(vmem_limit_bytes=4 * MIB),
+        name="cut",
+    )(
+        jnp.reshape(seq_index, (1,)),
+        *[pltpu.with_memory_space_constraint(a, pltpu.HBM) for a in (frames_in, *weights)],
+    )
 
 
 def make_kernel(dims, first, slot_counts):
@@ -66,6 +112,7 @@
     q_base = bank_n + LEFT
     q_rows = rows + RIGHT + PAD_ROWS
     scale = float(hd) ** (-0.5)
+    half = kv_rows // 2 // PAD_ROWS * PAD_ROWS
 
     def kernel(*refs):
         refs = list(refs)
@@ -73,21 +120,19 @@
         len_ref = refs.pop(0)
         if first:
             frames_ref, left_ref, right_ref, bank_ref = refs[:4]
-            refs = refs[4:]
-            w_refs = refs[:3]
-            refs = refs[3:]
-            ctx_ref, mem_ref, x_ref = refs[:3]
-            refs = refs[3:]
+            w_hbm = refs[4:7]
+            ctx_ref, mem_ref, x_hbm = refs[7:10]
+            k_scr, v_scr, q_scr, o_scr, m_scr, out_sem, x_ref, w_scr, in_sem = refs[10:]
         else:
-            x_ref = refs.pop(0)
+            x_hbm = refs.pop(0)
             w_refs = refs[: len(slot_counts)]
             refs = refs[len(slot_counts) + 2 :]
             ctx_ref, mem_ref = refs[:2]
-            refs = refs[2:]
-        k_scr, v_scr, q_scr, o_scr, m_scr, in_sem, out_sem = refs
-        col = scal_ref[0]
-        seq_index = scal_ref[1]
+            k_scr, v_scr, q_scr, o_scr, m_scr, out_sem, x_ref, in_sem = refs[2:]
+        seq_index = scal_ref[0]
+        col_at = pl.multiple_of(scal_ref[1] * cols, cols)
         row_base = seq_index * rows
+        waits = []
 
         if first:
             copies = []
@@ -102,13 +147,17 @@
                 ):
                     copies.append(
                         pltpu.make_async_copy(
-                            src.at[u], x_ref.at[u, pl.ds(at, size)], in_sem.at[u, n]
+                            src.at[u], x_ref.at[u, pl.ds(at, size)], in_sem.at[3 + 4 * u + n]
                         )
                     )
+            copies += [
+                pltpu.make_async_copy(w_hbm[n], w_scr.at[n], in_sem.at[n]) for n in range(3)
+            ]
             for c in copies:
                 c.start()
-            for c in copies:
+            for c in copies[:-3]:
                 c.wait()
+            arriving = {n: copies[n - 3] for n in range(3)}
             for u in range(utts):
                 length = len_ref[u]
                 seg_of = lax.broadcasted_iota(jnp.int32, (PAD_ROWS, rows), 0)
@@ -124,15 +173,30 @@
                 count = jnp.clip(length - (row_base + seg * seg_len), 1, seg_len)
                 mean = sums / count.astype(jnp.float32)
                 x_ref[u, q_base + rows + RIGHT :, :] = mean.astype(jnp.bfloat16)
+            done = pltpu.make_async_copy(x_ref, x_hbm, in_sem.at[3])
+            done.start()
+            waits.append(done)
+        else:
+            pieces = []
+            for u in range(utts):
+                for n, (lo, hi) in enumerate(((0, half), (half, kv_rows + PAD_ROWS))):
+                    pieces.append(
+                        pltpu.make_async_copy(
+                            x_hbm.at[u, pl.ds(lo, hi - lo)],
+                            x_ref.at[u, pl.ds(lo, hi - lo)],
+                            in_sem.at[2 * u + n],
+                        )
+                    )
+            for c in pieces:
+                c.start()
 
         lane = lax.broadcasted_iota(jnp.int32, (1, LANES), 1)
-        waits = []
         for u in range(utts):
             length = len_ref[u]
 
             def project(which, lo, size):
-                if first or len(slot_counts) == 1 and slot_counts[0] == 0:
-                    w = w_refs[which][...] if first else w_refs[0][which]
+                if first or slot_counts == (0,):
+                    w = w_scr[which] if first else w_refs[0][which]
                     return jnp.dot(
                         x_ref[u, lo : lo + size, :], w, preferred_element_type=jnp.float32
                     )
@@ -155,8 +219,20 @@
                     acc = part if acc is None else acc + part
                 return acc
 
-            k_scr[u] = project(1, 0, kv_rows).astype(jnp.bfloat16)
+            if first:
+                if u == 0:
+                    arriving[1].wait()
+                k_scr[u] = project(1, 0, kv_rows).astype(jnp.bfloat16)
+            else:
+                pieces[2 * u].wait()
+                k_scr[u, :half] = project(1, 0, half).astype(jnp.bfloat16)
+                pieces[2 * u + 1].wait()
+                k_scr[u, half:] = project(1, half, kv_rows - half).astype(jnp.bfloat16)
+            if first and u == 0:
+                arriving[2].wait()
             v_scr[u] = project(2, 0, kv_rows).astype(jnp.bfloat16)
+            if first and u == 0:
+                arriving[0].wait()
             q_scr[u] = project(0, q_base, q_rows).astype(jnp.bfloat16)
             n_key = bank_n + span
             key_at = lax.broadcasted_iota(jnp.int32, (1, n_key), 1)
@@ -225,12 +301,20 @@
                     m_scr[u, s : s + 1, at : at + LANES] = out[seg_len + s : seg_len + s + 1]
                 done = pltpu.make_async_copy(
                     o_scr.at[u, pl.ds(s * seg_len, seg_len)],
-                    ctx_ref.at[u, pl.ds(s * seg_len, seg_len), pl.ds(pl.multiple_of(col * cols, LANES), cols)],
+                    ctx_ref.at[u, pl.ds(s * seg_len, seg_len), pl.ds(col_at, cols)],
                     out_sem.at[u, s],
                 )
                 done.start()
                 waits.append(done)
-        mem_ref[...] = m_scr[...].astype(jnp.bfloat16)
+        o_scr[:, rows : rows + segs, :] = m_scr[...].astype(jnp.bfloat16)
+        for u in range(utts):
+            done = pltpu.make_async_copy(
+                o_scr.at[u, pl.ds(rows, segs)],
+                mem_ref.at[u, :, pl.ds(col_at, cols)],
+                out_sem.at[u, segs],
+            )
+            done.start()
+            waits.append(done)
         for done in waits:
             done.wait()
 
@@ -238,7 +322,7 @@
 
 
 def attend_chunk(dims, first, scal, lengths, inputs, weights, previous):
-    utts, rows, feat, cols, segs, seg_len, bank_n = dims
+    utts, rows, feat, cols, segs, _, bank_n = dims
     kv_rows = bank_n + LEFT + rows + RIGHT
     q_rows = rows + RIGHT + PAD_ROWS
     x_rows = kv_rows + PAD_ROWS
@@ -246,48 +330,58 @@
     if not first and weights[0].ndim == 3:
         slot_counts = (0,)
     anywhere = pl.BlockSpec(memory_space=pl.ANY)
-    whole = pl.BlockSpec(memory_space=pltpu.VMEM)
-    mem_block = pl.BlockSpec((utts, segs, cols), lambda i, s, n: (0, 0, s[0]))
+    vmem = pl.BlockSpec(memory_space=pltpu.VMEM)
+    smem = pl.BlockSpec(memory_space=pltpu.SMEM)
     ctx_shape = jax.ShapeDtypeStruct((utts, rows, feat), jnp.bfloat16)
     mem_shape = jax.ShapeDtypeStruct((utts, segs, feat), jnp.bfloat16)
     if first:
-        in_specs = [anywhere] * 4 + [whole] * len(weights)
-        args = list(inputs) + list(weights)
-        out_specs = [anywhere, mem_block, whole]
+        weights = [pltpu.with_memory_space_constraint(w, pltpu.HBM) for w in weights]
+    else:
+        inputs = [pltpu.with_memory_space_constraint(x, pltpu.HBM) for x in inputs]
+    args = [scal, lengths] + list(inputs) + list(weights) + list(previous)
+    scratch = [
+        pltpu.VMEM((utts, kv_rows, cols), jnp.bfloat16),
+        pltpu.VMEM((utts, kv_rows, cols), jnp.bfloat16),
+        pltpu.VMEM((utts, q_rows, cols), jnp.bfloat16),
+        pltpu.VMEM((utts, rows + PAD_ROWS, cols), jnp.bfloat16),
+        pltpu.VMEM((utts, segs, cols), jnp.float32),
+        pltpu.SemaphoreType.DMA((utts, segs + 1)),
+        pltpu.VMEM((utts, x_rows, feat), jnp.bfloat16),
+    ]
+    hbm = pl.BlockSpec(memory_space=pltpu.HBM)
+    if first:
+        in_specs = [smem] * 2 + [anywhere] * 4 + [hbm] * 3
+        out_specs = [anywhere, anywhere, hbm]
         out_shape = [
             ctx_shape,
             mem_shape,
-            jax.ShapeDtypeStruct((utts, x_rows, feat), jnp.bfloat16),
+            pltpu.HBM((utts, x_rows, feat), jnp.bfloat16),
         ]
         aliases = {}
+        scratch += [
+            pltpu.VMEM((3, feat, cols), jnp.bfloat16),
+            pltpu.SemaphoreType.DMA((3 + 4 * utts,)),
+        ]
     else:
-        in_specs = [whole] * (1 + len(weights)) + [anywhere] * 2
-        args = list(inputs) + list(weights) + list(previous)
-        out_specs = [anywhere, mem_block]
+        scratch.append(pltpu.SemaphoreType.DMA((2 * utts,)))
+        in_specs = [smem] * 2 + [hbm] + [vmem] * len(weights) + [anywhere] * 2
+        out_specs = [anywhere, anywhere]
         out_shape = [ctx_shape, mem_shape]
-        aliases = {len(args): 0, len(args) + 1: 1}
+        aliases = {len(args) - 2: 0, len(args) - 1: 1}
+    work = 2 * utts * (2 * kv_rows + q_rows) * feat * cols
     return pl.pallas_call(
         make_kernel(dims, first, slot_counts),
-        grid_spec=pltpu.PrefetchScalarGridSpec(
-            num_scalar_prefetch=2,
-            grid=(1,),
-            in_specs=in_specs,
-            out_specs=out_specs,
-            scratch_shapes=[
-                pltpu.VMEM((utts, kv_rows, cols), jnp.bfloat16),
-                pltpu.VMEM((utts, kv_rows, cols), jnp.bfloat16),
-                pltpu.VMEM((utts, q_rows, cols), jnp.bfloat16),
-                pltpu.VMEM((utts, rows, cols), jnp.bfloat16),
-                pltpu.VMEM((utts, segs, cols), jnp.float32),
-                pltpu.SemaphoreType.DMA((utts, 4)),
-                pltpu.SemaphoreType.DMA((utts, segs)),
-            ],
+        in_specs=in_specs,
+        out_specs=out_specs,
+        out_shape=out_shape,
+        scratch_shapes=scratch,
+        input_output_aliases=aliases,
+        compiler_params=pltpu.CompilerParams(vmem_limit_bytes=16 * MIB),
+        cost_estimate=pl.CostEstimate(
+            flops=4 * work, transcendentals=0, bytes_accessed=utts * x_rows * feat * 2
         ),
-        out_shape=out_shape,
-        input_output_aliases=aliases,
-        compiler_params=pltpu.CompilerParams(vmem_limit_bytes=20 * 1024 * 1024),
         name="attend_first" if first else "attend_next",
-    )(scal, lengths, *args)
+    )(*args)
 
 
 def local(frames_in, memory_in, w_query, w_key, w_value, lengths):
@@ -305,21 +399,17 @@
     dims = (utts, rows, feat, cols, segs, seg_len, bank_n)
 
     later = []
+    weights = (w_query, w_key, w_value)
     if sliced:
-        mine = jnp.stack(
-            [
-                lax.dynamic_slice_in_dim(w, seq_index * part, part, 0)
-                for w in (w_query, w_key, w_value)
-            ]
-        )
-        arrived = [
-            lax.ppermute(mine, "dp", [(i, i ^ r) for i in range(dp_count)])
-            for r in range(1, dp_count)
-        ]
+        mine, last, head = cut(seq_index, part, frames_in, weights)
+        arrived = {0: mine}
         for r in range(1, dp_count):
-            buffers, slots = gather_slices(arrived[r - 1], "seq")
+            low = r & -r
+            arrived[r] = swapped(arrived[r ^ low], "dp", (low, low))
+        for r in range(1, dp_count):
+            buffers, slots = gather_slices(arrived[r], "seq")
             later.append((dp_index ^ r, slots, buffers))
-        own = (dp_index, (w_query, w_key, w_value))
+        own = (dp_index, weights)
     else:
         full = [lax.all_gather(w, "dp", axis=1, tiled=True) for w in (w_query, w_key, w_value)]
         chunks = [
@@ -327,13 +417,15 @@
         ]
         own = chunks[0]
         later = [(c, [], [jnp.stack(ws)]) for c, ws in chunks[1:]]
-
-    left = shifted(frames_in[:, rows - LEFT :], "seq", 1)
-    right = shifted(frames_in[:, :RIGHT], "seq", -1)
-    bank, _ = gather_bank(memory_in, "seq")
+        last = frames_in[:, rows - LEFT :]
+        head = frames_in[:, :RIGHT]
+
+    left = shifted(last, "seq", 1)
+    right = shifted(head, "seq", -1)
+    bank = gather_bank(memory_in, "seq")
 
     def scalars(source, slots):
-        return jnp.stack([jnp.asarray(v, jnp.int32) for v in [source, seq_index] + list(slots)])
+        return jnp.stack([jnp.asarray(v, jnp.int32) for v in [seq_index, source] + list(slots)])
 
     context, memory_out, x_all = attend_chunk(
         dims,
@@ -346,7 +438,13 @@
     )
     for source, slots, buffers in later:
         context, memory_out = attend_chunk(
-            dims, False, scalars(source, slots), lengths, (x_all,), buffers, (context, memory_out)
+            dims,
+            False,
+            scalars(source, slots),
+            lengths,
+            (x_all,),
+            buffers,
+            (context, memory_out),
         )
     return context, memory_out
 

time: 94 us -> 71.2 us (0.76)
  the two profiles are of different devices: /device:TPU:3 before, /device:TPU:0 now
where the time goes in v2:
time: 71.2 us; the launch traced here: 70.9 us
  Pallas kernels  29.4 us (41%)
  starting transfers between devices  21.5 us (30%)
  waiting for transfers between devices  16 us (22%)
  other arithmetic  2.09 us (3%)
  between operations  1.62 us (2%)
    pallas_call x4, Pallas kernels, attend_chunk(): pl.pallas_call(make_kernel(dims, first, slot_counts), in_specs=in_specs,...  28.3 us
    ppermute x18, starting transfers between devices, swapped(): lax.ppermute(block, axis, [(i, i ^ masks[i % 2]) for i in range(count)])  17.8 us
    ppermute x18, waiting for transfers between devices, swapped(): lax.ppermute(block, axis, [(i, i ^ masks[i % 2]) for i in range(count)])  16 us
    ppermute x2, starting transfers between devices, shifted(): return lax.ppermute(block, axis, route)  3.71 us
    concatenate x3, other arithmetic, gather_slices(): sent = jnp.concatenate([block[0] for block in blocks], axis=0)  1.97 us
  transfers between devices with their start and end apart: 20, of which 5 were waited for; matrix products, arithmetic and copies ran while one was open for 3% of the time, Pallas kernels for 30%

profile of v2, /device:TPU:0, one launch (start us, length us, event | category | flops | bytes accessed | tf_op | source)
XLA Modules:
  0.0 70.9 jit_solution(10036951116667183315)
XLA Ops:
  0.6 1.1 %cut.1 = (bf16[3,128,256]{2,1,0:T(8,128)(2,1)S(1)}, bf16[1,128,1024]{2,1,0:T(8,128)(2,1)S(1)}, bf16[1,32,1024]{2,1,0:T(8,128)(2,1)S(1)}) custom-call(s32[1]{0:T(128)} %bitcast.scal_ref, bf16[1,512,1024]{2,1,0:T(8,128)(2,1)} %refs_2_.3, bf16[1024,256]{1,0:T(8,128)(2,1)} %refs_6_.1, bf16[1024,256]{1,0:T(8,128)(2,1)} %refs_7_.1, bf16[1024,256]{1,0:T(8,128)(2,1)} %refs_8_.1), custom_call_target="tpu_custom_call" | custom-call | tf_op jit(solution)/shard_map/cut/pallas_call | solution.py:88
  1.8 3.1 %collective-permute-start.15 = (bf16[3,128,256]{2,1,0:T(8,128)(2,1)S(1)}, bf16[3,128,256]{2,1,0:T(8,128)(2,1)S(1)}, u32[]{:S(2)}, u32[]{:S(2)}) collective-permute-start(bf16[3,128,256]{2,1,0:T(8,128)(2,1)S(1)} %get-tuple-element.15), channel_id=1, source_target_pairs={{0,8},{8,0},{16,24},{24,16},{1,9},{9,1},{17,25},{25,17},{2,10},{10... | collective-permute-start | bytes 589832 | tf_op jit(solution)/shard_map/ppermute | solution.py:26
  4.9 2.6 %collective-permute-start.5 = (bf16[3,128,256]{2,1,0:T(8,128)(2,1)S(1)}, bf16[3,128,256]{2,1,0:T(8,128)(2,1)}, u32[]{:S(2)}, u32[]{:S(2)}) collective-permute-start(bf16[3,128,256]{2,1,0:T(8,128)(2,1)S(1)} %get-tuple-element.15), channel_id=1, source_target_pairs={{0,16},{8,24},{16,0},{24,8},{1,17},{9,25},{17,1},{25,9},{2,18},{10... | collective-permute-start | bytes 589832 | tf_op jit(solution)/shard_map/ppermute | solution.py:26
  7.5 6.4 %collective-permute-done.15 = bf16[3,128,256]{2,1,0:T(8,128)(2,1)S(1)} collective-permute-done((bf16[3,128,256]{2,1,0:T(8,128)(2,1)S(1)}, bf16[3,128,256]{2,1,0:T(8,128)(2,1)S(1)}, u32[]{:S(2)}, u32[]{:S(2)}) %collective-permute-start.15) | collective-permute-done | bytes 196640 | tf_op jit(solution)/shard_map/ppermute | solution.py:26
  13.9 1.7 %collective-permute-start.16 = (bf16[1,3,128,256]{3,2,1,0:T(8,128)(2,1)S(1)}, bf16[1,3,128,256]{3,2,1,0:T(8,128)(2,1)S(1)}, u32[]{:S(2)}, u32[]{:S(2)}) collective-permute-start(bf16[1,3,128,256]{3,2,1,0:T(8,128)(2,1)S(1)} %bitcast.17), channel_id=1, source_target_pairs={{0,2},{1,5},{2,0},{3,7},{4,6},{5,1},{6,4},{7,3},{8,10},{9,13},{10,... | collective-permute-start | bytes 589832 | tf_op jit(solution)/shard_map/ppermute | solution.py:26
  15.6 2.4 %collective-permute-start = (bf16[1,128,1024]{2,1,0:T(8,128)(2,1)S(1)}, bf16[1,128,1024]{2,1,0:T(8,128)(2,1)S(1)}, u32[]{:S(2)}, u32[]{:S(2)}) collective-permute-start(bf16[1,128,1024]{2,1,0:T(8,128)(2,1)S(1)} %get-tuple-element.12), channel_id=1, source_target_pairs={{0,1},{1,2},{2,3},{3,4},{4,5},{5,6},{6,7},{8,9},{9,10},{10,11},{11... | collective-permute-start | bytes 786440 | tf_op jit(solution)/shard_map/ppermute | solution.py:21
  18.0 0.4 collective-permute-start.11
  18.4 1.7 %collective-permute-start.3 = (bf16[1,8,1024]{2,1,0:T(8,128)(2,1)S(1)}, bf16[1,8,1024]{2,1,0:T(8,128)(2,1)S(1)}, u32[]{:S(2)}, u32[]{:S(2)}) collective-permute-start(bf16[1,8,1024]{2,1,0:T(8,128)(2,1)S(1)} %pad_maximum_fusion.5), channel_id=1, source_target_pairs={{0,2},{1,3},{2,0},{3,1},{4,6},{5,7},{6,4},{7,5},{8,10},{9,11},{10,... | collective-permute-start | bytes 49160 | tf_op jit(solution)/shard_map/ppermute | solution.py:26
  20.2 1.6 %collective-permute-start.17 = (bf16[2,3,128,256]{3,2,1,0:T(8,128)(2,1)S(1)}, bf16[2,3,128,256]{3,2,1,0:T(8,128)(2,1)S(1)}, u32[]{:S(2)}, u32[]{:S(2)}) collective-permute-start(bf16[2,3,128,256]{3,2,1,0:T(8,128)(2,1)S(1)} %pad_maximum_fusion.2.refs_3_), channel_id=1, source_target_pairs={{0,4},{1,3},{2,6},{3,1},{4,0},{5,7},{6,2},{7,5},{8,12},{9,11},{10,... | collective-permute-start | bytes 1179656 | tf_op jit(solution)/shard_map/ppermute | solution.py:26
  21.8 4.3 %collective-permute-done.11 = bf16[1,3,128,256]{3,2,1,0:T(8,128)(2,1)S(1)} collective-permute-done((bf16[1,3,128,256]{3,2,1,0:T(8,128)(2,1)}, bf16[1,3,128,256]{3,2,1,0:T(8,128)(2,1)S(1)}, u32[]{:S(2)}, u32[]{:S(2)}) %collective-permute-start.11) | collective-permute-done | bytes 196640 | tf_op jit(solution)/shard_map/ppermute | solution.py:26
  26.0 1.0 %pad_maximum_fusion.1.refs_3_ = bf16[2,3,128,256]{3,2,1,0:T(8,128)(2,1)S(1)} fusion(bf16[1,3,128,256]{3,2,1,0:T(8,128)(2,1)S(1)} %collective-permute-done.11, bf16[1,3,128,256]{3,2,1,0:T(8,128)(2,1)} %bitcast.12), kind=kLoop, calls=%fused_computation.1 | loop fusion | flops 196608 | bytes 786432 | tf_op jit(solution)/shard_map/concatenate | solution.py:47
  27.5 1.6 %collective-permute-start.7 = (bf16[1,3,128,256]{3,2,1,0:T(8,128)(2,1)S(1)}, bf16[1,3,128,256]{3,2,1,0:T(8,128)(2,1)}, u32[]{:S(2)}, u32[]{:S(2)}) collective-permute-start(bf16[1,3,128,256]{3,2,1,0:T(8,128)(2,1)S(1)} %bitcast.15), channel_id=1, source_target_pairs={{0,2},{1,5},{2,0},{3,7},{4,6},{5,1},{6,4},{7,3},{8,10},{9,13},{10,... | collective-permute-start | bytes 589832 | tf_op jit(solution)/shard_map/ppermute | solution.py:26
  30.1 1.3 %collective-permute-start.1 = (bf16[1,32,1024]{2,1,0:T(8,128)(2,1)S(1)}, bf16[1,32,1024]{2,1,0:T(8,128)(2,1)S(1)}, u32[]{:S(2)}, u32[]{:S(2)}) collective-permute-start(bf16[1,32,1024]{2,1,0:T(8,128)(2,1)S(1)} %get-tuple-element.13), channel_id=1, source_target_pairs={{1,0},{2,1},{3,2},{4,3},{5,4},{6,5},{7,6},{9,8},{10,9},{11,10},{12... | collective-permute-start | bytes 196616 | tf_op jit(solution)/shard_map/ppermute | solution.py:21
  31.4 3.9 %collective-permute-done.7 = bf16[1,3,128,256]{3,2,1,0:T(8,128)(2,1)} collective-permute-done((bf16[1,3,128,256]{3,2,1,0:T(8,128)(2,1)S(1)}, bf16[1,3,128,256]{3,2,1,0:T(8,128)(2,1)}, u32[]{:S(2)}, u32[]{:S(2)}) %collective-permute-start.7) | collective-permute-done | bytes 196640 | tf_op jit(solution)/shard_map/ppermute | solution.py:26
  35.4 1.7 %collective-permute-start.4 = (bf16[1,16,1024]{2,1,0:T(8,128)(2,1)S(1)}, bf16[1,16,1024]{2,1,0:T(8,128)(2,1)S(1)}, u32[]{:S(2)}, u32[]{:S(2)}) collective-permute-start(bf16[1,16,1024]{2,1,0:T(8,128)(2,1)S(1)} %pad_maximum_fusion.4), channel_id=1, source_target_pairs={{0,4},{1,5},{2,6},{3,7},{4,0},{5,1},{6,2},{7,3},{8,12},{9,13},{10,... | collective-permute-start | bytes 98312 | tf_op jit(solution)/shard_map/ppermute | solution.py:26
  37.1 1.0 %pad_maximum_fusion.refs_3_ = bf16[2,3,128,256]{3,2,1,0:T(8,128)(2,1)S(1)} fusion(bf16[1,3,128,256]{3,2,1,0:T(8,128)(2,1)} %collective-permute-done.7, bf16[1,3,128,256]{3,2,1,0:T(8,128)(2,1)S(1)} %bitcast.16), kind=kLoop, calls=%fused_computation | loop fusion | flops 196608 | bytes 786432 | tf_op jit(solution)/shard_map/concatenate | solution.py:47
  38.1 1.2 %collective-permute-done.4 = bf16[1,16,1024]{2,1,0:T(8,128)(2,1)S(1)} collective-permute-done((bf16[1,16,1024]{2,1,0:T(8,128)(2,1)S(1)}, bf16[1,16,1024]{2,1,0:T(8,128)(2,1)S(1)}, u32[]{:S(2)}, u32[]{:S(2)}) %collective-permute-start.4) | collective-permute-done | bytes 32800 | tf_op jit(solution)/shard_map/ppermute | solution.py:26
  39.3 1.7 %collective-permute-start.8 = (bf16[2,3,128,256]{3,2,1,0:T(8,128)(2,1)S(1)}, bf16[2,3,128,256]{3,2,1,0:T(8,128)(2,1)S(1)}, u32[]{:S(2)}, u32[]{:S(2)}) collective-permute-start(bf16[2,3,128,256]{3,2,1,0:T(8,128)(2,1)S(1)} %pad_maximum_fusion.refs_3_), channel_id=1, source_target_pairs={{0,4},{1,3},{2,6},{3,1},{4,0},{5,7},{6,2},{7,5},{8,12},{9,11},{10,... | collective-permute-start | bytes 1179656 | tf_op jit(solution)/shard_map/ppermute | solution.py:26
  41.2 0.4 collective-permute-start.13
  41.8 8.2 %attend_first.1 = (bf16[1,512,1024]{2,1,0:T(8,128)(2,1)}, bf16[1,4,1024]{2,1,0:T(4,128)(2,1)}, bf16[1,720,1024]{2,1,0:T(8,128)(2,1)}) custom-call(s32[2]{0:T(128)S(1)} %pad_add_fusion.refs_0_, s32[1]{0:T(128)S(6)} %copy.20.refs_1_, bf16[1,512,1024]{2,1,0:T(8,128)(2,1)S(1)} %copy-done, bf16[1,128,1024]{2,1,0:T(8,128)(2,1)S(1)} %collective-permute-done.refs_3_, ...), custom_call_target="tpu_custom_call" | custom-call | flops 4127195136 | bytes 1474560 | tf_op jit(solution)/shard_map/attend_first/pallas_call | solution.py:372
  49.9 0.4 collective-permute-start.9
  50.5 6.6 %attend_next.3 = (bf16[1,512,1024]{2,1,0:T(8,128)(2,1)}, bf16[1,4,1024]{2,1,0:T(4,128)(2,1)}) custom-call(s32[10]{0:T(128)S(1)} %stack.83.refs_0_, s32[1]{0:T(128)S(6)} %copy.20.refs_1_, bf16[1,720,1024]{2,1,0:T(8,128)(2,1)} %get-tuple-element.14.refs_2_, ...), custom_call_target="tpu_custom_call", output_to_operand_aliasing={{0}: (7, {}), {1}: (8, {})} | custom-call | flops 4127195136 | bytes 1474560 | tf_op jit(solution)/shard_map/attend_next/pallas_call | solution.py:372
  57.2 6.6 %attend_next.4 = (bf16[1,512,1024]{2,1,0:T(8,128)(2,1)}, bf16[1,4,1024]{2,1,0:T(4,128)(2,1)}) custom-call(s32[10]{0:T(128)S(1)} %stack.81.refs_0_, s32[1]{0:T(128)S(6)} %copy.20.refs_1_, bf16[1,720,1024]{2,1,0:T(8,128)(2,1)} %get-tuple-element.14.refs_2_, ...), custom_call_target="tpu_custom_call", output_to_operand_aliasing={{0}: (7, {}), {1}: (8, {})} | custom-call | flops 4127195136 | bytes 1474560 | tf_op jit(solution)/shard_map/attend_next/pallas_call | solution.py:372
  63.9 6.9 %attend_next.5 = (bf16[1,512,1024]{2,1,0:T(8,128)(2,1)}, bf16[1,4,1024]{2,1,0:T(4,128)(2,1)}) custom-call(s32[10]{0:T(128)S(1)} %stack.77.refs_0_, s32[1]{0:T(128)S(6)} %copy.20.refs_1_, bf16[1,720,1024]{2,1,0:T(8,128)(2,1)} %get-tuple-element.14.refs_2_, ...), custom_call_target="tpu_custom_call", output_to_operand_aliasing={{0}: (7, {}), {1}: (8, {})} | custom-call | flops 4127195136 | bytes 1474560 | tf_op jit(solution)/shard_map/attend_next/pallas_call | solution.py:372
  (35 shorter events, 1.4 us)
Async XLA Ops:
  0.6 14.9 %copy-start.1 = (bf16[1,4,1024]{2,1,0:T(4,128)(2,1)S(1)}, bf16[1,4,1024]{2,1,0:T(4,128)(2,1)}, u32[]{:S(2)}) copy-start(bf16[1,4,1024]{2,1,0:T(4,128)(2,1)} %param.7) | copy-start | bytes 24580
  1.8 40.0 %copy-start = (bf16[1,512,1024]{2,1,0:T(8,128)(2,1)S(1)}, bf16[1,512,1024]{2,1,0:T(8,128)(2,1)}, u32[]{:S(2)}) copy-start(bf16[1,512,1024]{2,1,0:T(8,128)(2,1)} %refs_2_.3) | copy-start | bytes 3145732
  1.8 12.1 %collective-permute-start.15 = (bf16[3,128,256]{2,1,0:T(8,128)(2,1)S(1)}, bf16[3,128,256]{2,1,0:T(8,128)(2,1)S(1)}, u32[]{:S(2)}, u32[]{:S(2)}) collective-permute-start(bf16[3,128,256]{2,1,0:T(8,128)(2,1)S(1)} %get-tuple-element.15), channel_id=1, source_target_pairs={{0,8},{8,0},{16,24},{24,16},{1,9},{9,1},{17,25},{25,17},{2,10},{10... | collective-permute-start | bytes 589832 | tf_op jit(solution)/shard_map/ppermute | solution.py:26
  4.9 13.1 %collective-permute-start.5 = (bf16[3,128,256]{2,1,0:T(8,128)(2,1)S(1)}, bf16[3,128,256]{2,1,0:T(8,128)(2,1)}, u32[]{:S(2)}, u32[]{:S(2)}) collective-permute-start(bf16[3,128,256]{2,1,0:T(8,128)(2,1)S(1)} %get-tuple-element.15), channel_id=1, source_target_pairs={{0,16},{8,24},{16,0},{24,8},{1,17},{9,25},{17,1},{25,9},{2,18},{10... | collective-permute-start | bytes 589832 | tf_op jit(solution)/shard_map/ppermute | solution.py:26
  13.9 6.3 %collective-permute-start.16 = (bf16[1,3,128,256]{3,2,1,0:T(8,128)(2,1)S(1)}, bf16[1,3,128,256]{3,2,1,0:T(8,128)(2,1)S(1)}, u32[]{:S(2)}, u32[]{:S(2)}) collective-permute-start(bf16[1,3,128,256]{3,2,1,0:T(8,128)(2,1)S(1)} %bitcast.17), channel_id=1, source_target_pairs={{0,2},{1,5},{2,0},{3,7},{4,6},{5,1},{6,4},{7,3},{8,10},{9,13},{10,... | collective-permute-start | bytes 589832 | tf_op jit(solution)/shard_map/ppermute | solution.py:26
  15.5 2.9 %collective-permute-start.2 = (bf16[1,4,1024]{2,1,0:T(4,128)(2,1)S(1)}, bf16[1,4,1024]{2,1,0:T(4,128)(2,1)S(1)}, u32[]{:S(2)}, u32[]{:S(2)}) collective-permute-start(bf16[1,4,1024]{2,1,0:T(4,128)(2,1)S(1)} %copy-done.1), channel_id=1, source_target_pairs={{0,1},{1,0},{2,3},{3,2},{4,5},{5,4},{6,7},{7,6},{8,9},{9,8},{10,11... | collective-permute-start | bytes 24584 | tf_op jit(solution)/shard_map/ppermute | solution.py:26
  15.6 25.6 %collective-permute-start = (bf16[1,128,1024]{2,1,0:T(8,128)(2,1)S(1)}, bf16[1,128,1024]{2,1,0:T(8,128)(2,1)S(1)}, u32[]{:S(2)}, u32[]{:S(2)}) collective-permute-start(bf16[1,128,1024]{2,1,0:T(8,128)(2,1)S(1)} %get-tuple-element.12), channel_id=1, source_target_pairs={{0,1},{1,2},{2,3},{3,4},{4,5},{5,6},{6,7},{8,9},{9,10},{10,11},{11... | collective-permute-start | bytes 786440 | tf_op jit(solution)/shard_map/ppermute | solution.py:21
  18.0 8.1 %collective-permute-start.11 = (bf16[1,3,128,256]{3,2,1,0:T(8,128)(2,1)}, bf16[1,3,128,256]{3,2,1,0:T(8,128)(2,1)S(1)}, u32[]{:S(2)}, u32[]{:S(2)}) collective-permute-start(bf16[1,3,128,256]{3,2,1,0:T(8,128)(2,1)} %bitcast.12), channel_id=1, source_target_pairs={{0,2},{1,5},{2,0},{3,7},{4,6},{5,1},{6,4},{7,3},{8,10},{9,13},{10,... | collective-permute-start | bytes 589832 | tf_op jit(solution)/shard_map/ppermute | solution.py:26
  18.4 11.7 %collective-permute-start.3 = (bf16[1,8,1024]{2,1,0:T(8,128)(2,1)S(1)}, bf16[1,8,1024]{2,1,0:T(8,128)(2,1)S(1)}, u32[]{:S(2)}, u32[]{:S(2)}) collective-permute-start(bf16[1,8,1024]{2,1,0:T(8,128)(2,1)S(1)} %pad_maximum_fusion.5), channel_id=1, source_target_pairs={{0,2},{1,3},{2,0},{3,1},{4,6},{5,7},{6,4},{7,5},{8,10},{9,11},{10,... | collective-permute-start | bytes 49160 | tf_op jit(solution)/shard_map/ppermute | solution.py:26
  20.2 7.3 %collective-permute-start.6 = (bf16[3,128,256]{2,1,0:T(8,128)(2,1)}, bf16[3,128,256]{2,1,0:T(8,128)(2,1)S(1)}, u32[]{:S(2)}, u32[]{:S(2)}) collective-permute-start(bf16[3,128,256]{2,1,0:T(8,128)(2,1)} %collective-permute-done.5), channel_id=1, source_target_pairs={{0,8},{8,0},{16,24},{24,16},{1,9},{9,1},{17,25},{25,17},{2,10},{10... | collective-permute-start | bytes 589832 | tf_op jit(solution)/shard_map/ppermute | solution.py:26
  20.2 20.8 %collective-permute-start.17 = (bf16[2,3,128,256]{3,2,1,0:T(8,128)(2,1)S(1)}, bf16[2,3,128,256]{3,2,1,0:T(8,128)(2,1)S(1)}, u32[]{:S(2)}, u32[]{:S(2)}) collective-permute-start(bf16[2,3,128,256]{3,2,1,0:T(8,128)(2,1)S(1)} %pad_maximum_fusion.2.refs_3_), channel_id=1, source_target_pairs={{0,4},{1,3},{2,6},{3,1},{4,0},{5,7},{6,2},{7,5},{8,12},{9,11},{10,... | collective-permute-start | bytes 1179656 | tf_op jit(solution)/shard_map/ppermute | solution.py:26
  27.0 14.6 %collective-permute-start.12 = (bf16[2,3,128,256]{3,2,1,0:T(8,128)(2,1)S(1)}, bf16[2,3,128,256]{3,2,1,0:T(8,128)(2,1)S(1)}, u32[]{:S(2)}, u32[]{:S(2)}) collective-permute-start(bf16[2,3,128,256]{3,2,1,0:T(8,128)(2,1)S(1)} %pad_maximum_fusion.1.refs_3_), channel_id=1, source_target_pairs={{0,4},{1,3},{2,6},{3,1},{4,0},{5,7},{6,2},{7,5},{8,12},{9,11},{10,... | collective-permute-start | bytes 1179656 | tf_op jit(solution)/shard_map/ppermute | solution.py:26
  27.5 7.9 %collective-permute-start.7 = (bf16[1,3,128,256]{3,2,1,0:T(8,128)(2,1)S(1)}, bf16[1,3,128,256]{3,2,1,0:T(8,128)(2,1)}, u32[]{:S(2)}, u32[]{:S(2)}) collective-permute-start(bf16[1,3,128,256]{3,2,1,0:T(8,128)(2,1)S(1)} %bitcast.15), channel_id=1, source_target_pairs={{0,2},{1,5},{2,0},{3,7},{4,6},{5,1},{6,4},{7,3},{8,10},{9,13},{10,... | collective-permute-start | bytes 589832 | tf_op jit(solution)/shard_map/ppermute | solution.py:26
  30.1 9.2 %collective-permute-start.1 = (bf16[1,32,1024]{2,1,0:T(8,128)(2,1)S(1)}, bf16[1,32,1024]{2,1,0:T(8,128)(2,1)S(1)}, u32[]{:S(2)}, u32[]{:S(2)}) collective-permute-start(bf16[1,32,1024]{2,1,0:T(8,128)(2,1)S(1)} %get-tuple-element.13), channel_id=1, source_target_pairs={{1,0},{2,1},{3,2},{4,3},{5,4},{6,5},{7,6},{9,8},{10,9},{11,10},{12... | collective-permute-start | bytes 196616 | tf_op jit(solution)/shard_map/ppermute | solution.py:21
  35.4 3.9 %collective-permute-start.4 = (bf16[1,16,1024]{2,1,0:T(8,128)(2,1)S(1)}, bf16[1,16,1024]{2,1,0:T(8,128)(2,1)S(1)}, u32[]{:S(2)}, u32[]{:S(2)}) collective-permute-start(bf16[1,16,1024]{2,1,0:T(8,128)(2,1)S(1)} %pad_maximum_fusion.4), channel_id=1, source_target_pairs={{0,4},{1,5},{2,6},{3,7},{4,0},{5,1},{6,2},{7,3},{8,12},{9,13},{10,... | collective-permute-start | bytes 98312 | tf_op jit(solution)/shard_map/ppermute | solution.py:26
  39.3 10.7 %collective-permute-start.18 = (bf16[2,3,128,256]{3,2,1,0:T(8,128)(2,1)S(1)}, bf16[2,3,128,256]{3,2,1,0:T(8,128)(2,1)S(1)}, u32[]{:S(2)}, u32[]{:S(2)}) collective-permute-start(bf16[2,3,128,256]{3,2,1,0:T(8,128)(2,1)S(1)} %pad_maximum_fusion.2.refs_3_), channel_id=1, source_target_pairs={{0,1},{1,0},{2,3},{3,2},{4,5},{5,4},{6,7},{7,6},{8,9},{9,8},{10,11... | collective-permute-start | bytes 1179656 | tf_op jit(solution)/shard_map/ppermute | solution.py:26
  39.3 11.1 %collective-permute-start.8 = (bf16[2,3,128,256]{3,2,1,0:T(8,128)(2,1)S(1)}, bf16[2,3,128,256]{3,2,1,0:T(8,128)(2,1)S(1)}, u32[]{:S(2)}, u32[]{:S(2)}) collective-permute-start(bf16[2,3,128,256]{3,2,1,0:T(8,128)(2,1)S(1)} %pad_maximum_fusion.refs_3_), channel_id=1, source_target_pairs={{0,4},{1,3},{2,6},{3,1},{4,0},{5,7},{6,2},{7,5},{8,12},{9,11},{10,... | collective-permute-start | bytes 1179656 | tf_op jit(solution)/shard_map/ppermute | solution.py:26
  41.0 9.5 %collective-permute-start.19 = (bf16[2,3,128,256]{3,2,1,0:T(8,128)(2,1)S(1)}, bf16[2,3,128,256]{3,2,1,0:T(8,128)(2,1)S(1)}, u32[]{:S(2)}, u32[]{:S(2)}) collective-permute-start(bf16[2,3,128,256]{3,2,1,0:T(8,128)(2,1)S(1)} %collective-permute-done.17.refs_4_), channel_id=1, source_target_pairs={{0,1},{1,0},{2,3},{3,2},{4,5},{5,4},{6,7},{7,6},{8,9},{9,8},{10,11... | collective-permute-start | bytes 1179656 | tf_op jit(solution)/shard_map/ppermute | solution.py:26
  41.2 16.0 %collective-permute-start.13 = (bf16[2,3,128,256]{3,2,1,0:T(8,128)(2,1)S(1)}, bf16[2,3,128,256]{3,2,1,0:T(8,128)(2,1)S(1)}, u32[]{:S(2)}, u32[]{:S(2)}) collective-permute-start(bf16[2,3,128,256]{3,2,1,0:T(8,128)(2,1)S(1)} %pad_maximum_fusion.1.refs_3_), channel_id=1, source_target_pairs={{0,1},{1,0},{2,3},{3,2},{4,5},{5,4},{6,7},{7,6},{8,9},{9,8},{10,11... | collective-permute-start | bytes 1179656 | tf_op jit(solution)/shard_map/ppermute | solution.py:26
  41.6 15.6 %collective-permute-start.14 = (bf16[2,3,128,256]{3,2,1,0:T(8,128)(2,1)S(1)}, bf16[2,3,128,256]{3,2,1,0:T(8,128)(2,1)S(1)}, u32[]{:S(2)}, u32[]{:S(2)}) collective-permute-start(bf16[2,3,128,256]{3,2,1,0:T(8,128)(2,1)S(1)} %collective-permute-done.12.refs_4_), channel_id=1, source_target_pairs={{0,1},{1,0},{2,3},{3,2},{4,5},{5,4},{6,7},{7,6},{8,9},{9,8},{10,11... | collective-permute-start | bytes 1179656 | tf_op jit(solution)/shard_map/ppermute | solution.py:26
  49.9 13.9 %collective-permute-start.9 = (bf16[2,3,128,256]{3,2,1,0:T(8,128)(2,1)S(1)}, bf16[2,3,128,256]{3,2,1,0:T(8,128)(2,1)S(1)}, u32[]{:S(2)}, u32[]{:S(2)}) collective-permute-start(bf16[2,3,128,256]{3,2,1,0:T(8,128)(2,1)S(1)} %pad_maximum_fusion.refs_3_), channel_id=1, source_target_pairs={{0,1},{1,0},{2,3},{3,2},{4,5},{5,4},{6,7},{7,6},{8,9},{9,8},{10,11... | collective-permute-start | bytes 1179656 | tf_op jit(solution)/shard_map/ppermute | solution.py:26
  50.4 13.5 %collective-permute-start.10 = (bf16[2,3,128,256]{3,2,1,0:T(8,128)(2,1)S(1)}, bf16[2,3,128,256]{3,2,1,0:T(8,128)(2,1)S(1)}, u32[]{:S(2)}, u32[]{:S(2)}) collective-permute-start(bf16[2,3,128,256]{3,2,1,0:T(8,128)(2,1)S(1)} %collective-permute-done.8.refs_4_), channel_id=1, source_target_pairs={{0,1},{1,0},{2,3},{3,2},{4,5},{5,4},{6,7},{7,6},{8,9},{9,8},{10,11... | collective-permute-start | bytes 1179656 | tf_op jit(solution)/shard_map/ppermute | solution.py:26

commit v3 on v0

v3 whole, which is shorter than its diff:
```python
import math

import jax
import jax.numpy as jnp
from jax import lax
from jax.experimental import pallas as pl
from jax.experimental.pallas import tpu as pltpu
from jax.sharding import PartitionSpec as P


HEADS = 16
LEFT = 128
RIGHT = 32
LANES = 128
PAD_ROWS = 16
DEAD = -1e30
MIB = 1024 * 1024


def shifted(block, axis, distance):
    count = lax.axis_size(axis)
    route = [(i - distance, i) for i in range(count) if 0 <= i - distance < count]
    return lax.ppermute(block, axis, route)


def swapped(block, axis, masks):
    count = lax.axis_size(axis)
    return lax.ppermute(block, axis, [(i, i ^ masks[i % 2]) for i in range(count)])


def stage_masks(count):
    bits = [1 << b for b in range(1, count.bit_length() - 1)]
    turned = bits[1:] + bits[:1]
    return [pair for pair in zip(bits, turned)] + [(1, 1)]


def joined(parts):
    rows = sum(p.shape[0] for p in parts)
    out = jnp.zeros((rows,) + parts[0].shape[1:], parts[0].dtype)
    at = 0
    for p in parts:
        out = lax.dynamic_update_slice_in_dim(out, p, at, 0)
        at += p.shape[0]
    return out


def gather_slices(mine, axis, tail=None):
    (even_a, odd_a), (even_b, odd_b) = stage_masks(lax.axis_size(axis))[:2]
    size = mine.shape[0]
    sent = mine if tail is None else joined([mine, tail])
    got = swapped(sent, axis, (even_a, odd_a))
    both = [mine, got] if tail is None else [mine, got[:size], tail, got[size:]]
    held = joined(both)
    other = swapped(held, axis, (even_b, odd_b))
    pair_held = swapped(held, axis, (1, 1))
    pair_other = swapped(other, axis, (1, 1))
    slots = [(0, 0), (even_a, odd_a), (even_b, odd_b), (even_a ^ even_b, odd_a ^ odd_b)]
    slots += [(o ^ 1, e ^ 1) for e, o in slots]
    return [held, other, pair_held, pair_other], slots


def gather_bank(memory_in, axis):
    count = lax.axis_size(axis)
    bank = memory_in
    bit = 1
    while bit < count:
        bank = jnp.concatenate([bank, swapped(bank, axis, (bit, bit))], axis=1)
        bit *= 2
    return bank


def cut(ids, part, frames_in, memory_in, weights):
    _, rows, feat = frames_in.shape
    segs = memory_in.shape[1]
    cols = weights[0].shape[1]
    groups = feat // cols
    packed = part // groups

    def kernel(scal_ref, f_ref, m_ref, *refs):
        w_refs = refs[:3]
        u_ref, near_ref, far_ref, m_scr, sem = refs[3:]
        at = pl.multiple_of(scal_ref[0] * part, part)
        odd = scal_ref[0] % 2
        copies = []
        for n, w in enumerate(w_refs):
            for g in range(groups):
                copies.append(
                    pltpu.make_async_copy(
                        w.at[pl.ds(at + g * packed, packed)],
                        u_ref.at[pl.ds(n * packed, packed), pl.ds(g * cols, cols)],
                        sem.at[n * groups + g],
                    )
                )
        top = pl.multiple_of((rows - LEFT) * odd, PAD_ROWS)
        end = pl.multiple_of((rows - LEFT) * (1 - odd), PAD_ROWS)
        copies.append(
            pltpu.make_async_copy(
                f_ref.at[0, pl.ds(end, LEFT)], near_ref.at[pl.ds(0, LEFT)], sem.at[3 * groups]
            )
        )
        copies.append(
            pltpu.make_async_copy(f_ref.at[0, pl.ds(top, LEFT)], far_ref, sem.at[3 * groups + 1])
        )
        copies.append(pltpu.make_async_copy(m_ref.at[0], m_scr, sem.at[3 * groups + 2]))
        for c in copies:
            c.start()
        for c in copies:
            c.wait()
        near_ref[LEFT : LEFT + segs, :] = m_scr[...]
        near_ref[LEFT + segs :, :] = jnp.zeros((PAD_ROWS - segs, feat), jnp.bfloat16)

    hbm = pl.BlockSpec(memory_space=pltpu.HBM)
    vmem = pl.BlockSpec(memory_space=pltpu.VMEM)
    return pl.pallas_call(
        kernel,
        in_specs=[pl.BlockSpec(memory_space=pltpu.SMEM)] + [hbm] * 5,
        out_specs=[vmem] * 3,
        out_shape=[
            jax.ShapeDtypeStruct((3 * packed, feat), jnp.bfloat16),
            jax.ShapeDtypeStruct((LEFT + PAD_ROWS, feat), jnp.bfloat16),
            jax.ShapeDtypeStruct((LEFT, feat), jnp.bfloat16),
        ],
        scratch_shapes=[
            pltpu.VMEM((segs, feat), jnp.bfloat16),
            pltpu.SemaphoreType.DMA((3 * groups + 3,)),
        ],
        compiler_params=pltpu.CompilerParams(vmem_limit_bytes=4 * MIB),
        name="cut",
    )(ids, *[in_hbm(a) for a in (frames_in, memory_in, *weights)])


def in_hbm(a):
    return pltpu.with_memory_space_constraint(a, pltpu.HBM)


def in_vmem(a):
    return pltpu.with_memory_space_constraint(a, pltpu.VMEM)


def attend_segment(q, k_main, k_tail, v_main, v_tail, main_bias, tail_bias, hd):
    n_q, cols = q.shape
    heads = cols // hd
    tail_n = k_tail.shape[0]
    scale = float(hd) ** (-0.5)
    exact = math.frexp(scale)[0] == 0.5
    if exact:
        q = q * jnp.asarray(scale, q.dtype)
    lane_head = lax.broadcasted_iota(jnp.int32, (1, cols), 1) // hd
    tail_head = lax.broadcasted_iota(jnp.int32, (1, heads * tail_n), 1) // tail_n

    def only(a, h):
        return jnp.where(lane_head == h, a, jnp.zeros_like(a))

    def split(a):
        return [a[:, j : j + LANES] for j in range(0, a.shape[1], LANES)]

    def folded(parts, op):
        out = parts[0]
        for part in parts[1:]:
            out = op(out, part)
        return out

    across = (((1,), (1,)), ((), ()))
    main = lax.dot_general(
        jnp.concatenate([only(q, h) for h in range(heads)], axis=0),
        k_main,
        across,
        preferred_element_type=jnp.float32,
    )
    tail = lax.dot_general(
        q,
        jnp.concatenate([only(k_tail, h) for h in range(heads)], axis=0),
        across,
        preferred_element_type=jnp.float32,
    )
    if not exact:
        main = main * scale
        tail = tail * scale
    tails = split(tail + tail_bias)
    owners = split(tail_head)
    held = [
        [j for j in range(len(tails)) if j * LANES < (h + 1) * tail_n and (j + 1) * LANES > h * tail_n]
        for h in range(heads)
    ]
    tops = []
    probs = []
    for h in range(heads):
        scores = main[h * n_q : (h + 1) * n_q] + main_bias
        parts = split(scores) + [jnp.where(owners[j] == h, tails[j], DEAD) for j in held[h]]
        top = jnp.max(folded(parts, jnp.maximum), axis=-1, keepdims=True)
        tops.append(top)
        probs.append(jnp.exp(scores - top))
    tail_probs = []
    for j, block in enumerate(tails):
        inside = [h for h in range(heads) if j in held[h]]
        top = tops[inside[0]]
        for h in inside[1:]:
            top = jnp.where(owners[j] >= h, tops[h], top)
        tail_probs.append(jnp.exp(block - top))
    shares = []
    for h in range(heads):
        parts = split(probs[h]) + [jnp.where(owners[j] == h, tail_probs[j], 0.0) for j in held[h]]
        shares.append(1.0 / jnp.sum(folded(parts, jnp.add), axis=-1, keepdims=True))
    mixed = jnp.dot(
        jnp.concatenate([p.astype(jnp.bfloat16) for p in probs + tail_probs], axis=1),
        jnp.concatenate(
            [only(v_main, h) for h in range(heads)] + [only(v_tail, h) for h in range(heads)],
            axis=0,
        ),
        preferred_element_type=jnp.float32,
    )
    outs = []
    for block, head in zip(split(mixed), split(lane_head)):
        at = len(outs) * LANES
        inside = [h for h in range(heads) if at <= h * hd < at + LANES]
        share = shares[inside[0]]
        for h in inside[1:]:
            share = jnp.where(head >= h, shares[h], share)
        outs.append(block * share)
    return jnp.concatenate(outs, axis=1)


def make_kernel(dims, first, last, sliced, n_buffers, columns, bank_devices, slots):
    utts, rows, feat, cols, segs, seg_len, bank_n = dims
    hd = feat // HEADS
    heads = cols // hd
    main_n = LEFT + seg_len
    tail_n = bank_n + RIGHT
    kv_rows = bank_n + LEFT + rows + RIGHT
    q_base = bank_n + LEFT
    n_slots = len(slots)
    n_before = len(columns) - 1 if last else 0

    def kernel(*refs):
        refs = list(refs)

        def take(n):
            got = refs[:n]
            del refs[:n]
            return got

        ids_ref, len_ref = take(2)
        if first:
            (frames_ref,) = take(1)
            edges = take(4 if sliced else 3)
            w_hbm = take(3)
        else:
            (x_ref,) = take(1)
            w_refs = take(n_buffers)
        before = take(n_before)
        if last:
            ctx_ref, mem_ref = take(2)
        else:
            (o_ref,) = take(1)
        if first:
            (x_ref,) = take(1)
        k_scr, v_scr, q_scr, m_scr = take(4)
        if first:
            w_scr, in_sem = take(2)
        if last:
            o_ref, out_sem = take(2)
        seq_index = ids_ref[0]
        odd = seq_index % 2 == 1
        row_base = seq_index * rows
        waits = []

        def column(which):
            kind, value = columns[which]
            index = ids_ref[1] ^ value if kind == "xor" else value
            return pl.multiple_of(index * cols, cols)

        def device(pair):
            return seq_index ^ jnp.where(odd, pair[1], pair[0])

        def write_out(block_ref, at, u, lo, size, target, sem):
            done = pltpu.make_async_copy(
                block_ref.at[u, pl.ds(lo, size)],
                target.at[u, pl.ds(0 if target is mem_ref else lo, size), pl.ds(at, cols)],
                sem,
            )
            done.start()
            waits.append(done)

        for n, block_ref in enumerate(before):
            for u in range(utts):
                write_out(block_ref, column(n), u, 0, rows, ctx_ref, out_sem.at[u, 2 * n])
                write_out(
                    block_ref, column(n), u, rows, segs, mem_ref, out_sem.at[u, 2 * n + 1]
                )

        if first:
            loads = [pltpu.make_async_copy(w_hbm[n], w_scr.at[n], in_sem.at[n]) for n in range(3)]
            moves = [
                pltpu.make_async_copy(
                    frames_ref.at[u], x_ref.at[u, pl.ds(q_base, rows)], in_sem.at[3 + u]
                )
                for u in range(utts)
            ]
            for c in moves + [loads[1], loads[2], loads[0]]:
                c.start()
            if sliced:
                near_ref, far_ref, held_ref, other_ref = edges
                near = near_ref[:LEFT, :]
                far = far_ref[...]
                x_ref[0, bank_n:q_base, :] = jnp.where(odd, near, far)
                x_ref[0, q_base + rows : kv_rows, :] = jnp.where(odd, far[:RIGHT], near[:RIGHT])
                x_ref[0, : bank_n // 2, :] = held_ref[held_ref.shape[0] - bank_n // 2 :, :]
                x_ref[0, bank_n // 2 : bank_n, :] = other_ref[other_ref.shape[0] - bank_n // 2 :, :]
            else:
                left_ref, right_ref, bank_ref = edges
                x_ref[:, bank_n:q_base, :] = left_ref[...]
                x_ref[:, q_base + rows : kv_rows, :] = right_ref[...]
                x_ref[:, :bank_n, :] = bank_ref[...]
            for c in moves:
                c.wait()
            for u in range(utts):
                length = len_ref[u]
                seg_of = lax.broadcasted_iota(jnp.int32, (PAD_ROWS, rows), 0)
                pos = lax.broadcasted_iota(jnp.int32, (PAD_ROWS, rows), 1)
                pick = (pos // seg_len == seg_of) & (row_base + pos < length)
                sums = jnp.dot(
                    jnp.where(pick, 1.0, 0.0).astype(jnp.bfloat16),
                    x_ref[u, q_base : q_base + rows, :],
                    preferred_element_type=jnp.float32,
                )
                seg = lax.broadcasted_iota(jnp.int32, (PAD_ROWS, 1), 0)
                count = jnp.clip(length - (row_base + seg * seg_len), 1, seg_len)
                mean = sums / count.astype(jnp.float32)
                x_ref[u, kv_rows:, :] = mean.astype(jnp.bfloat16)

        tail_at = lax.broadcasted_iota(jnp.int32, (1, heads * tail_n), 1) % tail_n
        block = tail_at // segs
        entry = tail_at % segs
        for b, pair in enumerate(bank_devices):
            entry = entry + jnp.where(block == b, device(pair) * segs, 0)
        main_at = lax.broadcasted_iota(jnp.int32, (1, main_n), 1)

        for u in range(utts):
            length = len_ref[u]

            def project(which, lo, hi):
                if first or n_slots == 0:
                    if first and u == 0:
                        loads[which].wait()
                    w = w_scr[which] if first else w_refs[0][which]
                    return jnp.dot(
                        x_ref[u, lo:hi, :], w, preferred_element_type=jnp.float32
                    ).astype(jnp.bfloat16)
                part = feat // n_slots
                packed = part * cols // feat
                per = n_slots // n_buffers
                acc = None
                for t in range(0, n_slots, 2):
                    lhs = []
                    rhs = []
                    for s in (t, t + 1):
                        at = pl.multiple_of(device(slots[s]) * part, LANES)
                        lhs.append(x_ref[u, lo:hi, pl.ds(at, part)])
                        top = (s % per * 3 + which) * packed
                        for g in range(0, feat, cols):
                            rhs.append(w_refs[s // per][top : top + packed, g : g + cols])
                    one = jnp.dot(
                        jnp.concatenate(lhs, axis=1),
                        jnp.concatenate(rhs, axis=0),
                        preferred_element_type=jnp.float32,
                    )
                    acc = one if acc is None else acc + one
                return acc.astype(jnp.bfloat16)

            k_scr[u] = project(1, 0, kv_rows)
            v_scr[u] = project(2, 0, kv_rows)
            q_scr[u] = project(0, q_base, kv_rows + PAD_ROWS)
            for s in range(segs):
                seg_index = seq_index * segs + s
                start = row_base + s * seg_len
                main_pos = start - LEFT + main_at
                main_bias = jnp.where((main_pos >= 0) & (main_pos < length), 0.0, DEAD)
                bank_live = (tail_at < bank_n) & (entry < seg_index) & (entry * seg_len < length)
                right_pos = start + seg_len - bank_n + tail_at
                tail_live = bank_live | ((tail_at >= bank_n) & (right_pos < length))
                tail_bias = jnp.where(tail_live, 0.0, DEAD)
                win = bank_n + s * seg_len
                edge = win + main_n

                def keys(scr):
                    both = [scr[u, :bank_n, :], scr[u, edge : edge + RIGHT, :]]
                    return scr[u, win:edge, :], jnp.concatenate(both, axis=0)

                k_main, k_tail = keys(k_scr)
                v_main, v_tail = keys(v_scr)
                q = jnp.concatenate(
                    [q_scr[u, s * seg_len : (s + 1) * seg_len, :], q_scr[u, rows + RIGHT :, :]],
                    axis=0,
                )
                out = attend_segment(
                    q, k_main, k_tail, v_main, v_tail, main_bias, tail_bias, hd
                )
                row_at = lax.broadcasted_iota(jnp.int32, (seg_len, 1), 0)
                live = jnp.where(start + row_at < length, out[:seg_len], 0.0)
                o_ref[u, s * seg_len : (s + 1) * seg_len, :] = live.astype(jnp.bfloat16)
                m_scr[u, s : s + 1, :] = out[seg_len + s : seg_len + s + 1]
                if last:
                    write_out(
                        o_ref,
                        column(-1),
                        u,
                        s * seg_len,
                        seg_len,
                        ctx_ref,
                        out_sem.at[u, 2 * n_before + s],
                    )
            o_ref[u, rows : rows + segs, :] = m_scr[u].astype(jnp.bfloat16)
            if last:
                write_out(
                    o_ref, column(-1), u, rows, segs, mem_ref, out_sem.at[u, 2 * n_before + segs]
                )
        for done in waits:
            done.wait()

    return kernel


def attend_chunk(
    dims, sliced, first, last, scalars, inputs, weights, columns, bank_devices, slots, before=()
):
    utts, rows, feat, cols, segs, _, bank_n = dims
    kv_rows = bank_n + LEFT + rows + RIGHT
    q_rows = rows + RIGHT + PAD_ROWS
    block = (utts, rows + PAD_ROWS, cols)
    anywhere = pl.BlockSpec(memory_space=pl.ANY)
    hbm = pl.BlockSpec(memory_space=pltpu.HBM)
    vmem = pl.BlockSpec(memory_space=pltpu.VMEM)
    smem = pl.BlockSpec(memory_space=pltpu.SMEM)
    if first:
        weights = [in_hbm(w) for w in weights]
    else:
        inputs = [in_vmem(x) for x in inputs]
        before = [in_vmem(b) for b in before]
    args = [*scalars, *inputs, *weights, *before]
    scratch = [
        pltpu.VMEM((utts, kv_rows, cols), jnp.bfloat16),
        pltpu.VMEM((utts, kv_rows, cols), jnp.bfloat16),
        pltpu.VMEM((utts, q_rows, cols), jnp.bfloat16),
        pltpu.VMEM((utts, segs, cols), jnp.float32),
    ]
    in_specs = [smem] * 2
    if first:
        in_specs += [anywhere] + [vmem] * (len(inputs) - 1) + [hbm] * 3
        scratch += [
            pltpu.VMEM((3, feat, cols), jnp.bfloat16),
            pltpu.SemaphoreType.DMA((3 + utts,)),
        ]
    else:
        in_specs += [vmem] * (1 + len(weights))
    in_specs += [vmem] * len(before)
    if last:
        out_specs = [anywhere] * 2
        out_shape = [
            jax.ShapeDtypeStruct((utts, rows, feat), jnp.bfloat16),
            jax.ShapeDtypeStruct((utts, segs, feat), jnp.bfloat16),
        ]
        scratch += [
            pltpu.VMEM(block, jnp.bfloat16),
            pltpu.SemaphoreType.DMA((utts, 2 * len(before) + segs + 1)),
        ]
    else:
        out_specs = [vmem]
        out_shape = [pltpu.VMEM(block, jnp.bfloat16)]
    if first:
        out_specs.append(vmem)
        out_shape.append(pltpu.VMEM((utts, kv_rows + PAD_ROWS, feat), jnp.bfloat16))
    work = 2 * utts * (2 * kv_rows + q_rows) * feat * cols
    return pl.pallas_call(
        make_kernel(dims, first, last, sliced, len(weights), columns, bank_devices, slots),
        in_specs=in_specs,
        out_specs=out_specs,
        out_shape=out_shape,
        scratch_shapes=scratch,
        compiler_params=pltpu.CompilerParams(vmem_limit_bytes=16 * MIB),
        cost_estimate=pl.CostEstimate(
            flops=4 * work, transcendentals=0, bytes_accessed=utts * kv_rows * feat * 2
        ),
        name="attend_first" if first else "attend_next",
    )(*args)


def local(frames_in, memory_in, w_query, w_key, w_value, lengths):
    utts, rows, feat = frames_in.shape
    segs = memory_in.shape[1]
    seg_len = rows // segs
    seq_count = lax.axis_size("seq")
    dp_count = lax.axis_size("dp")
    ids = jnp.stack([lax.axis_index("seq"), lax.axis_index("dp")]).astype(jnp.int32)
    bank_n = segs * seq_count
    part = feat // seq_count
    weights = (w_query, w_key, w_value)
    width = w_query.shape[1]
    sliced = (
        utts == 1
        and len(stage_masks(seq_count)) == 3
        and dp_count & (dp_count - 1) == 0
        and part % LANES == 0
        and width % LANES == 0
        and part * width // feat % PAD_ROWS == 0
        and 4 * segs % PAD_ROWS == 0
        and segs <= PAD_ROWS
        and RIGHT <= LEFT <= rows
    )
    cols = width if sliced else feat // 4
    dims = (utts, rows, feat, cols, segs, seg_len, bank_n)

    if sliced:
        mine, near_sent, far_sent = cut(ids, part, frames_in, memory_in, weights)
        arrived = {0: mine}
        arrived[1] = swapped(mine, "dp", (1, 1))
        near = swapped(near_sent, "seq", (1, 1))
        inner = [(i, i + 1) for i in range(1, seq_count - 1, 2)]
        far = lax.ppermute(far_sent, "seq", inner + [(b, a) for a, b in inner])
        for r in range(2, dp_count):
            low = r & -r
            arrived[r] = swapped(arrived[r ^ low], "dp", (low, low))
        pair_bank = jnp.concatenate([memory_in[0], near[LEFT : LEFT + segs]], axis=0)
        later = []
        for r in range(1, dp_count):
            buffers, slots = gather_slices(arrived[r], "seq", pair_bank if r == 1 else None)
            later.append((("xor", r), slots, buffers))
        own = (("xor", 0), weights)
        edges = (near, far, later[0][2][0], later[0][2][1])
        bank_devices = [(e ^ h, o ^ h) for e, o in later[0][1][:4] for h in (0, 1)]
    else:
        full = [lax.all_gather(w, "dp", axis=1, tiled=True) for w in weights]
        chunks = [
            (("at", c), [w[:, c * cols : (c + 1) * cols] for w in full]) for c in range(feat // cols)
        ]
        own = chunks[0]
        later = [(c, [], [jnp.stack(ws)]) for c, ws in chunks[1:]]
        left = shifted(frames_in[:, rows - LEFT :], "seq", 1)
        right = shifted(frames_in[:, :RIGHT], "seq", -1)
        edges = (left, right, gather_bank(memory_in, "seq"))
        bank_devices = [(t, t) for t in range(seq_count)]

    scalars = (ids, lengths)
    block, x_all = attend_chunk(
        dims,
        sliced,
        True,
        False,
        scalars,
        (frames_in, *edges),
        own[1],
        [own[0]],
        bank_devices,
        [],
    )
    blocks = [block]
    columns = [own[0]]
    for n, (source, slots, buffers) in enumerate(later):
        last = n == len(later) - 1
        columns.append(source)
        outs = attend_chunk(
            dims,
            sliced,
            False,
            last,
            scalars,
            (x_all,),
            buffers,
            list(columns),
            bank_devices,
            slots,
            blocks if last else (),
        )
        blocks.append(outs[0])
    return tuple(outs)


def solution(mesh):
    placed = (
        P("dp", "seq", None),
        P("dp", "seq", None),
        P(None, "dp"),
        P(None, "dp"),
        P(None, "dp"),
        P("dp"),
    )
    return jax.shard_map(
        local,
        mesh=mesh,
        in_specs=placed,
        out_specs=(P("dp", "seq", None), P("dp", "seq", None)),
        check_vma=False,
    )
```

time: 254 us -> 59.5 us (0.23)
  waiting for transfers between devices: 112 us -> 13.6 us
  local copies, waits for them, and re-layouts: 37.7 us -> 0.12 us
  matrix products: 33.9 us -> 0 us
  Pallas kernels: 0 us -> 21.1 us
  other arithmetic: 18.3 us -> 0.11 us
  loops' own time: 13.5 us -> 0 us
  between operations: 14.5 us -> 1.47 us
  blocking collectives: 9.73 us -> 0 us
  starting transfers between devices: 12.8 us -> 22.4 us
    all_gather x3 -> x0, waiting for transfers between devices: 109 us -> none  [the longest x1 38.7 us: local(): q_flat = project_one(lax.all_gather(w_query, 'dp', axis=1, tiled=True))]
    dot_general x8 -> x0, matrix products: 21.9 us -> none  [the longest x4 11.6 us: attend(): jnp.einsum('bhqk,bkhe->bqhe', weights, v_heads, preferred_element_type=jn...]
    pallas_call x0 -> x5, Pallas kernels: none -> 21.1 us  [the longest x4 19.2 us: attend_chunk(): pl.pallas_call(make_kernel(dims, first, last, sliced, len(weights), colum...]
    dynamic_slice x36 -> x0, local copies, waits for them, and re-layouts: 15.6 us -> none  [the longest x8 5.85 us: one_segment(): k_window = lax.dynamic_slice_in_dim(k_ext, seg_index * seg_len, key_span, 1)]
    another operation x1 -> x0, loops' own time: 13.5 us -> none  [local(): attended = lax.map(one_segment, jnp.arange(seg_dev, dtype=jnp.int32))]
    sub x4 -> x0, matrix products: 12.1 us -> none  [attend(): probs = jnp.exp(scores - row_max)]
    ppermute x4 -> x17, waiting for transfers between devices: 1.55 us -> 13.6 us  [the longest x16 13.6 us: swapped(): lax.ppermute(block, axis, [(i, i ^ masks[i % 2]) for i in range(count)])]
    concatenate x14 -> x0, other arithmetic: 11.7 us -> none  [the longest x4 7.31 us: one_segment(): values = jnp.concatenate([bank_values, v_window], axis=1)]
  transfers between devices with their start and end apart: 7 -> 17, of which waited for: 4 -> 4; matrix products, arithmetic and copies ran while one was open for 7% -> 0% of each run, Pallas kernels for 0% -> 24%
where the time goes in v3:
time: 59.5 us; the launch traced here: 58.8 us
  starting transfers between devices  22.4 us (38%)
  Pallas kernels  21.1 us (35%)
  waiting for transfers between devices  13.6 us (23%)
  between operations  1.47 us (2%)
    pallas_call x4, Pallas kernels, attend_chunk(): pl.pallas_call(make_kernel(dims, first, last, sliced, len(weights), colum...  19.2 us
    ppermute x16, starting transfers between devices, swapped(): lax.ppermute(block, axis, [(i, i ^ masks[i % 2]) for i in range(count)])  16.5 us
    ppermute x16, waiting for transfers between devices, swapped(): lax.ppermute(block, axis, [(i, i ^ masks[i % 2]) for i in range(count)])  13.6 us
    ppermute x1, starting transfers between devices, local(): far = lax.ppermute(far_sent, 'seq', inner + [(b, a) for a, b in inner])  5.96 us
    pallas_call x1, Pallas kernels, cut(): pl.pallas_call(kernel, in_specs=[pl.BlockSpec(memory_space=pltpu.SMEM)] +...  1.87 us
  transfers between devices with their start and end apart: 17, of which 4 were waited for; matrix products, arithmetic and copies ran while one was open for 0% of the time, Pallas kernels for 24%

profile of v3, /device:TPU:3, one launch (start us, length us, event | category | flops | bytes accessed | tf_op | source)
XLA Modules:
  0.0 58.8 jit_solution(1947203225762424387)
XLA Ops:
  0.7 1.9 %cut.1 = (bf16[96,1024]{1,0:T(8,128)(2,1)S(1)}, bf16[144,1024]{1,0:T(8,128)(2,1)S(1)}, bf16[128,1024]{1,0:T(8,128)(2,1)S(1)}) custom-call(s32[2]{0:T(128)S(1)} %pad_add_fusion.scal_ref.refs_0_, bf16[1,512,1024]{2,1,0:T(8,128)(2,1)} %refs_2_.3, bf16[1,4,1024]{2,1,0:T(4,128)(2,1)} %m_ref.1, bf16[1024,256]{1,0:T(8,128)(2,1)} %refs_7_.1, ...), custom_call_target="tpu_custom_call" | custom-call | tf_op jit(solution)/shard_map/cut/pallas_call | solution.py:114
  2.6 0.7 %collective-permute-start = (bf16[144,1024]{1,0:T(8,128)(2,1)S(1)}, bf16[144,1024]{1,0:T(8,128)(2,1)S(1)}, u32[]{:S(2)}, u32[]{:S(2)}) collective-permute-start(bf16[144,1024]{1,0:T(8,128)(2,1)S(1)} %get-tuple-element.7), channel_id=1, source_target_pairs={{0,1},{1,0},{2,3},{3,2},{4,5},{5,4},{6,7},{7,6},{8,9},{9,8},{10,11... | collective-permute-start | bytes 884744 | tf_op jit(solution)/shard_map/ppermute | solution.py:28
  3.3 1.3 %collective-permute-start.2 = (bf16[96,1024]{1,0:T(8,128)(2,1)S(1)}, bf16[96,1024]{1,0:T(8,128)(2,1)S(1)}, u32[]{:S(2)}, u32[]{:S(2)}) collective-permute-start(bf16[96,1024]{1,0:T(8,128)(2,1)S(1)} %get-tuple-element.9), channel_id=1, source_target_pairs={{0,8},{8,0},{16,24},{24,16},{1,9},{9,1},{17,25},{25,17},{2,10},{10... | collective-permute-start | bytes 589832 | tf_op jit(solution)/shard_map/ppermute | solution.py:28
  4.6 2.3 %collective-permute-start.5 = (bf16[96,1024]{1,0:T(8,128)(2,1)S(1)}, bf16[96,1024]{1,0:T(8,128)(2,1)S(1)}, u32[]{:S(2)}, u32[]{:S(2)}) collective-permute-start(bf16[96,1024]{1,0:T(8,128)(2,1)S(1)} %get-tuple-element.9), channel_id=1, source_target_pairs={{0,16},{8,24},{16,0},{24,8},{1,17},{9,25},{17,1},{25,9},{2,18},{10... | collective-permute-start | bytes 589832 | tf_op jit(solution)/shard_map/ppermute | solution.py:28
  7.0 6.9 %collective-permute-done.2 = bf16[96,1024]{1,0:T(8,128)(2,1)S(1)} collective-permute-done((bf16[96,1024]{1,0:T(8,128)(2,1)S(1)}, bf16[96,1024]{1,0:T(8,128)(2,1)S(1)}, u32[]{:S(2)}, u32[]{:S(2)}) %collective-permute-start.2) | collective-permute-done | bytes 196640 | tf_op jit(solution)/shard_map/ppermute | solution.py:28
  13.8 1.3 %collective-permute-start.3 = (bf16[104,1024]{1,0:T(8,128)(2,1)S(1)}, bf16[104,1024]{1,0:T(8,128)(2,1)S(1)}, u32[]{:S(2)}, u32[]{:S(2)}) collective-permute-start(bf16[104,1024]{1,0:T(8,128)(2,1)S(1)} %pad_maximum_fusion), channel_id=1, source_target_pairs={{0,2},{1,5},{2,0},{3,7},{4,6},{5,1},{6,4},{7,3},{8,10},{9,13},{10,... | collective-permute-start | bytes 638984 | tf_op jit(solution)/shard_map/ppermute | solution.py:28
  15.2 0.2 collective-permute-start.13
  15.4 2.1 %collective-permute-start.6 = (bf16[96,1024]{1,0:T(8,128)(2,1)S(1)}, bf16[96,1024]{1,0:T(8,128)(2,1)S(1)}, u32[]{:S(2)}, u32[]{:S(2)}) collective-permute-start(bf16[96,1024]{1,0:T(8,128)(2,1)S(1)} %collective-permute-done.5), channel_id=1, source_target_pairs={{0,8},{8,0},{16,24},{24,16},{1,9},{9,1},{17,25},{25,17},{2,10},{10... | collective-permute-start | bytes 589832 | tf_op jit(solution)/shard_map/ppermute | solution.py:28
  17.6 1.3 %collective-permute-done.3 = bf16[104,1024]{1,0:T(8,128)(2,1)S(1)} collective-permute-done((bf16[104,1024]{1,0:T(8,128)(2,1)S(1)}, bf16[104,1024]{1,0:T(8,128)(2,1)S(1)}, u32[]{:S(2)}, u32[]{:S(2)}) %collective-permute-start.3) | collective-permute-done | bytes 213024 | tf_op jit(solution)/shard_map/ppermute | solution.py:28
  19.0 0.4 collective-permute-start.4
  19.4 1.6 %collective-permute-done.13 = bf16[96,1024]{1,0:T(8,128)(2,1)S(1)} collective-permute-done((bf16[96,1024]{1,0:T(8,128)(2,1)S(1)}, bf16[96,1024]{1,0:T(8,128)(2,1)S(1)}, u32[]{:S(2)}, u32[]{:S(2)}) %collective-permute-start.13) | collective-permute-done | bytes 196640 | tf_op jit(solution)/shard_map/ppermute | solution.py:28
  21.0 0.4 collective-permute-start.14
  21.5 1.1 %collective-permute-start.7 = (bf16[96,1024]{1,0:T(8,128)(2,1)S(1)}, bf16[96,1024]{1,0:T(8,128)(2,1)S(1)}, u32[]{:S(2)}, u32[]{:S(2)}) collective-permute-start(bf16[96,1024]{1,0:T(8,128)(2,1)S(1)} %collective-permute-done.6), channel_id=1, source_target_pairs={{0,2},{1,5},{2,0},{3,7},{4,6},{5,1},{6,4},{7,3},{8,10},{9,13},{10,... | collective-permute-start | bytes 589832 | tf_op jit(solution)/shard_map/ppermute | solution.py:28
  22.6 6.0 %collective-permute-start.1 = (bf16[128,1024]{1,0:T(8,128)(2,1)S(1)}, bf16[128,1024]{1,0:T(8,128)(2,1)S(1)}, u32[]{:S(2)}, u32[]{:S(2)}) collective-permute-start(bf16[128,1024]{1,0:T(8,128)(2,1)S(1)} %get-tuple-element.8), channel_id=1, source_target_pairs={{1,2},{3,4},{5,6},{2,1},{4,3},{6,5},{9,10},{11,12},{13,14},{10,9},... | collective-permute-start | bytes 786440 | tf_op jit(solution)/shard_map/ppermute | solution.py:518
  28.7 0.9 %collective-permute-start.8 = (bf16[192,1024]{1,0:T(8,128)(2,1)S(1)}, bf16[192,1024]{1,0:T(8,128)(2,1)S(1)}, u32[]{:S(2)}, u32[]{:S(2)}) collective-permute-start(bf16[192,1024]{1,0:T(8,128)(2,1)S(1)} %constant_dynamic-update-slice_fusion.refs_3_), channel_id=1, source_target_pairs={{0,4},{1,3},{2,6},{3,1},{4,0},{5,7},{6,2},{7,5},{8,12},{9,11},{10,... | collective-permute-start | bytes 1179656 | tf_op jit(solution)/shard_map/ppermute | solution.py:28
  29.6 3.7 %collective-permute-done.14.refs_4_ = bf16[192,1024]{1,0:T(8,128)(2,1)S(1)} collective-permute-done((bf16[192,1024]{1,0:T(8,128)(2,1)S(1)}, bf16[192,1024]{1,0:T(8,128)(2,1)S(1)}, u32[]{:S(2)}, u32[]{:S(2)}) %collective-permute-start.14) | collective-permute-done | bytes 393248 | tf_op jit(solution)/shard_map/ppermute | solution.py:28
  33.3 4.4 %collective-permute-start.16 = (bf16[192,1024]{1,0:T(8,128)(2,1)S(1)}, bf16[192,1024]{1,0:T(8,128)(2,1)S(1)}, u32[]{:S(2)}, u32[]{:S(2)}) collective-permute-start(bf16[192,1024]{1,0:T(8,128)(2,1)S(1)} %collective-permute-done.14.refs_4_), channel_id=1, source_target_pairs={{0,1},{1,0},{2,3},{3,2},{4,5},{5,4},{6,7},{7,6},{8,9},{9,8},{10,11... | collective-permute-start | bytes 1179656 | tf_op jit(solution)/shard_map/ppermute | solution.py:28
  38.5 0.5 collective-permute-start.12
  39.0 6.1 %attend_first.1 = (bf16[1,528,256]{2,1,0:T(8,128)(2,1)S(1)}, bf16[1,720,1024]{2,1,0:T(8,128)(2,1)S(1)}) custom-call(s32[2]{0:T(128)S(1)} %pad_add_fusion.scal_ref.refs_0_, s32[1]{0:T(128)S(6)} %copy.13.refs_1_, bf16[1,512,1024]{2,1,0:T(8,128)(2,1)S(1)} %copy-done, bf16[144,1024]{1,0:T(8,128)(2,1)S(1)} %collective-permute-done.refs_3_, ...), custom_call_target="tpu_custom_call" | custom-call | flops 4127195136 | bytes 1441792 | tf_op jit(solution)/shard_map/attend_first/pallas_call | solution.py:473
  45.1 0.1 collective-permute-start.9
  45.3 0.4 collective-permute-start.10
  45.7 4.1 %attend_next.4.refs_9_ = bf16[1,528,256]{2,1,0:T(8,128)(2,1)S(1)} custom-call(s32[2]{0:T(128)S(1)} %pad_add_fusion.scal_ref.refs_0_, s32[1]{0:T(128)S(6)} %copy.13.refs_1_, bf16[1,720,1024]{2,1,0:T(8,128)(2,1)S(1)} %get-tuple-element.10.refs_2_, bf16[192,1024]{1,0:T(8,128)(2,1)S(1)} %constant_dynamic-update-slice_fusion.2.refs_3_, ...), custom_call_target="tpu_custom_call" | custom-call | flops 4127195136 | bytes 1441792 | tf_op jit(solution)/shard_map/attend_next/pallas_call | solution.py:473
  49.8 4.1 %attend_next.3.refs_8_ = bf16[1,528,256]{2,1,0:T(8,128)(2,1)S(1)} custom-call(s32[2]{0:T(128)S(1)} %pad_add_fusion.scal_ref.refs_0_, s32[1]{0:T(128)S(6)} %copy.13.refs_1_, bf16[1,720,1024]{2,1,0:T(8,128)(2,1)S(1)} %get-tuple-element.10.refs_2_, bf16[208,1024]{1,0:T(8,128)(2,1)S(1)} %slice_dynamic-update-slice_fusion.1.refs_5_.refs_3_, ...), custom_call_target="tpu_custom_call" | custom-call | flops 4127195136 | bytes 1441792 | tf_op jit(solution)/shard_map/attend_next/pallas_call | solution.py:473
  54.0 4.8 %attend_next.5 = (bf16[1,512,1024]{2,1,0:T(8,128)(2,1)}, bf16[1,4,1024]{2,1,0:T(4,128)(2,1)}) custom-call(s32[2]{0:T(128)S(1)} %pad_add_fusion.scal_ref.refs_0_, s32[1]{0:T(128)S(6)} %copy.13.refs_1_, bf16[1,720,1024]{2,1,0:T(8,128)(2,1)S(1)} %get-tuple-element.10.refs_2_, bf16[192,1024]{1,0:T(8,128)(2,1)S(1)} %constant_dynamic-update-slice_fusion.refs_3_, ...), custom_call_target="tpu_custom_call" | custom-call | flops 4127195136 | bytes 1441792 | tf_op jit(solution)/shard_map/attend_next/pallas_call | solution.py:473
  (30 shorter events, 0.4 us)
Async XLA Ops:
  0.6 13.2 %copy-start.1 = (bf16[1,4,1024]{2,1,0:T(4,128)(2,1)S(1)}, bf16[1,4,1024]{2,1,0:T(4,128)(2,1)}, u32[]{:S(2)}) copy-start(bf16[1,4,1024]{2,1,0:T(4,128)(2,1)} %m_ref.1) | copy-start | bytes 24580
  2.6 4.3 %collective-permute-start = (bf16[144,1024]{1,0:T(8,128)(2,1)S(1)}, bf16[144,1024]{1,0:T(8,128)(2,1)S(1)}, u32[]{:S(2)}, u32[]{:S(2)}) collective-permute-start(bf16[144,1024]{1,0:T(8,128)(2,1)S(1)} %get-tuple-element.7), channel_id=1, source_target_pairs={{0,1},{1,0},{2,3},{3,2},{4,5},{5,4},{6,7},{7,6},{8,9},{9,8},{10,11... | collective-permute-start | bytes 884744 | tf_op jit(solution)/shard_map/ppermute | solution.py:28
  3.3 10.5 %collective-permute-start.2 = (bf16[96,1024]{1,0:T(8,128)(2,1)S(1)}, bf16[96,1024]{1,0:T(8,128)(2,1)S(1)}, u32[]{:S(2)}, u32[]{:S(2)}) collective-permute-start(bf16[96,1024]{1,0:T(8,128)(2,1)S(1)} %get-tuple-element.9), channel_id=1, source_target_pairs={{0,8},{8,0},{16,24},{24,16},{1,9},{9,1},{17,25},{25,17},{2,10},{10... | collective-permute-start | bytes 589832 | tf_op jit(solution)/shard_map/ppermute | solution.py:28
  4.6 10.5 %collective-permute-start.5 = (bf16[96,1024]{1,0:T(8,128)(2,1)S(1)}, bf16[96,1024]{1,0:T(8,128)(2,1)S(1)}, u32[]{:S(2)}, u32[]{:S(2)}) collective-permute-start(bf16[96,1024]{1,0:T(8,128)(2,1)S(1)} %get-tuple-element.9), channel_id=1, source_target_pairs={{0,16},{8,24},{16,0},{24,8},{1,17},{9,25},{17,1},{25,9},{2,18},{10... | collective-permute-start | bytes 589832 | tf_op jit(solution)/shard_map/ppermute | solution.py:28
  13.8 25.1 %copy-start = (bf16[1,512,1024]{2,1,0:T(8,128)(2,1)S(1)}, bf16[1,512,1024]{2,1,0:T(8,128)(2,1)}, u32[]{:S(2)}) copy-start(bf16[1,512,1024]{2,1,0:T(8,128)(2,1)} %refs_2_.3) | copy-start | bytes 3145732
  13.8 5.1 %collective-permute-start.3 = (bf16[104,1024]{1,0:T(8,128)(2,1)S(1)}, bf16[104,1024]{1,0:T(8,128)(2,1)S(1)}, u32[]{:S(2)}, u32[]{:S(2)}) collective-permute-start(bf16[104,1024]{1,0:T(8,128)(2,1)S(1)} %pad_maximum_fusion), channel_id=1, source_target_pairs={{0,2},{1,5},{2,0},{3,7},{4,6},{5,1},{6,4},{7,3},{8,10},{9,13},{10,... | collective-permute-start | bytes 638984 | tf_op jit(solution)/shard_map/ppermute | solution.py:28
  15.2 5.9 %collective-permute-start.13 = (bf16[96,1024]{1,0:T(8,128)(2,1)S(1)}, bf16[96,1024]{1,0:T(8,128)(2,1)S(1)}, u32[]{:S(2)}, u32[]{:S(2)}) collective-permute-start(bf16[96,1024]{1,0:T(8,128)(2,1)S(1)} %collective-permute-done.5), channel_id=1, source_target_pairs={{0,2},{1,5},{2,0},{3,7},{4,6},{5,1},{6,4},{7,3},{8,10},{9,13},{10,... | collective-permute-start | bytes 589832 | tf_op jit(solution)/shard_map/ppermute | solution.py:28
  15.4 6.1 %collective-permute-start.6 = (bf16[96,1024]{1,0:T(8,128)(2,1)S(1)}, bf16[96,1024]{1,0:T(8,128)(2,1)S(1)}, u32[]{:S(2)}, u32[]{:S(2)}) collective-permute-start(bf16[96,1024]{1,0:T(8,128)(2,1)S(1)} %collective-permute-done.5), channel_id=1, source_target_pairs={{0,8},{8,0},{16,24},{24,16},{1,9},{9,1},{17,25},{25,17},{2,10},{10... | collective-permute-start | bytes 589832 | tf_op jit(solution)/shard_map/ppermute | solution.py:28
  19.0 19.5 %collective-permute-start.4 = (bf16[208,1024]{1,0:T(8,128)(2,1)S(1)}, bf16[208,1024]{1,0:T(8,128)(2,1)S(1)}, u32[]{:S(2)}, u32[]{:S(2)}) collective-permute-start(bf16[208,1024]{1,0:T(8,128)(2,1)S(1)} %slice_dynamic-update-slice_fusion.1.refs_5_.refs_3_), channel_id=1, source_target_pairs={{0,4},{1,3},{2,6},{3,1},{4,0},{5,7},{6,2},{7,5},{8,12},{9,11},{10,... | collective-permute-start | bytes 1277960 | tf_op jit(solution)/shard_map/ppermute | solution.py:28
  21.0 12.3 %collective-permute-start.14 = (bf16[192,1024]{1,0:T(8,128)(2,1)S(1)}, bf16[192,1024]{1,0:T(8,128)(2,1)S(1)}, u32[]{:S(2)}, u32[]{:S(2)}) collective-permute-start(bf16[192,1024]{1,0:T(8,128)(2,1)S(1)} %constant_dynamic-update-slice_fusion.2.refs_3_), channel_id=1, source_target_pairs={{0,4},{1,3},{2,6},{3,1},{4,0},{5,7},{6,2},{7,5},{8,12},{9,11},{10,... | collective-permute-start | bytes 1179656 | tf_op jit(solution)/shard_map/ppermute | solution.py:28
  21.5 7.2 %collective-permute-start.7 = (bf16[96,1024]{1,0:T(8,128)(2,1)S(1)}, bf16[96,1024]{1,0:T(8,128)(2,1)S(1)}, u32[]{:S(2)}, u32[]{:S(2)}) collective-permute-start(bf16[96,1024]{1,0:T(8,128)(2,1)S(1)} %collective-permute-done.6), channel_id=1, source_target_pairs={{0,2},{1,5},{2,0},{3,7},{4,6},{5,1},{6,4},{7,3},{8,10},{9,13},{10,... | collective-permute-start | bytes 589832 | tf_op jit(solution)/shard_map/ppermute | solution.py:28
  22.6 15.8 %collective-permute-start.1 = (bf16[128,1024]{1,0:T(8,128)(2,1)S(1)}, bf16[128,1024]{1,0:T(8,128)(2,1)S(1)}, u32[]{:S(2)}, u32[]{:S(2)}) collective-permute-start(bf16[128,1024]{1,0:T(8,128)(2,1)S(1)} %get-tuple-element.8), channel_id=1, source_target_pairs={{1,2},{3,4},{5,6},{2,1},{4,3},{6,5},{9,10},{11,12},{13,14},{10,9},... | collective-permute-start | bytes 786440 | tf_op jit(solution)/shard_map/ppermute | solution.py:518
  28.6 16.5 %collective-permute-start.15 = (bf16[192,1024]{1,0:T(8,128)(2,1)S(1)}, bf16[192,1024]{1,0:T(8,128)(2,1)S(1)}, u32[]{:S(2)}, u32[]{:S(2)}) collective-permute-start(bf16[192,1024]{1,0:T(8,128)(2,1)S(1)} %constant_dynamic-update-slice_fusion.2.refs_3_), channel_id=1, source_target_pairs={{0,1},{1,0},{2,3},{3,2},{4,5},{5,4},{6,7},{7,6},{8,9},{9,8},{10,11... | collective-permute-start | bytes 1179656 | tf_op jit(solution)/shard_map/ppermute | solution.py:28
  28.7 16.6 %collective-permute-start.8 = (bf16[192,1024]{1,0:T(8,128)(2,1)S(1)}, bf16[192,1024]{1,0:T(8,128)(2,1)S(1)}, u32[]{:S(2)}, u32[]{:S(2)}) collective-permute-start(bf16[192,1024]{1,0:T(8,128)(2,1)S(1)} %constant_dynamic-update-slice_fusion.refs_3_), channel_id=1, source_target_pairs={{0,4},{1,3},{2,6},{3,1},{4,0},{5,7},{6,2},{7,5},{8,12},{9,11},{10,... | collective-permute-start | bytes 1179656 | tf_op jit(solution)/shard_map/ppermute | solution.py:28
  33.3 12.4 %collective-permute-start.16 = (bf16[192,1024]{1,0:T(8,128)(2,1)S(1)}, bf16[192,1024]{1,0:T(8,128)(2,1)S(1)}, u32[]{:S(2)}, u32[]{:S(2)}) collective-permute-start(bf16[192,1024]{1,0:T(8,128)(2,1)S(1)} %collective-permute-done.14.refs_4_), channel_id=1, source_target_pairs={{0,1},{1,0},{2,3},{3,2},{4,5},{5,4},{6,7},{7,6},{8,9},{9,8},{10,11... | collective-permute-start | bytes 1179656 | tf_op jit(solution)/shard_map/ppermute | solution.py:28
  38.4 11.4 %collective-permute-start.11 = (bf16[208,1024]{1,0:T(8,128)(2,1)S(1)}, bf16[208,1024]{1,0:T(8,128)(2,1)S(1)}, u32[]{:S(2)}, u32[]{:S(2)}) collective-permute-start(bf16[208,1024]{1,0:T(8,128)(2,1)S(1)} %slice_dynamic-update-slice_fusion.1.refs_5_.refs_3_), channel_id=1, source_target_pairs={{0,1},{1,0},{2,3},{3,2},{4,5},{5,4},{6,7},{7,6},{8,9},{9,8},{10,11... | collective-permute-start | bytes 1277960 | tf_op jit(solution)/shard_map/ppermute | solution.py:28
  38.5 11.4 %collective-permute-start.12 = (bf16[208,1024]{1,0:T(8,128)(2,1)S(1)}, bf16[208,1024]{1,0:T(8,128)(2,1)S(1)}, u32[]{:S(2)}, u32[]{:S(2)}) collective-permute-start(bf16[208,1024]{1,0:T(8,128)(2,1)S(1)} %collective-permute-done.4.refs_6_.refs_4_), channel_id=1, source_target_pairs={{0,1},{1,0},{2,3},{3,2},{4,5},{5,4},{6,7},{7,6},{8,9},{9,8},{10,11... | collective-permute-start | bytes 1277960 | tf_op jit(solution)/shard_map/ppermute | solution.py:28
  45.1 8.9 %collective-permute-start.9 = (bf16[192,1024]{1,0:T(8,128)(2,1)S(1)}, bf16[192,1024]{1,0:T(8,128)(2,1)S(1)}, u32[]{:S(2)}, u32[]{:S(2)}) collective-permute-start(bf16[192,1024]{1,0:T(8,128)(2,1)S(1)} %constant_dynamic-update-slice_fusion.refs_3_), channel_id=1, source_target_pairs={{0,1},{1,0},{2,3},{3,2},{4,5},{5,4},{6,7},{7,6},{8,9},{9,8},{10,11... | collective-permute-start | bytes 1179656 | tf_op jit(solution)/shard_map/ppermute | solution.py:28
  45.3 8.7 %collective-permute-start.10 = (bf16[192,1024]{1,0:T(8,128)(2,1)S(1)}, bf16[192,1024]{1,0:T(8,128)(2,1)S(1)}, u32[]{:S(2)}, u32[]{:S(2)}) collective-permute-start(bf16[192,1024]{1,0:T(8,128)(2,1)S(1)} %collective-permute-done.8.refs_4_), channel_id=1, source_target_pairs={{0,1},{1,0},{2,3},{3,2},{4,5},{5,4},{6,7},{7,6},{8,9},{9,8},{10,11... | collective-permute-start | bytes 1179656 | tf_op jit(solution)/shard_map/ppermute | solution.py:28
